TPU v7x, 256 devices: a whole 4x4x8 slice. The times are simulated.
256 devices in a mesh: cube: 8 (over z_lo, core), row: 8 (over z_hi, x), col: 4 (over y).
Axes of the slice: x: 4, y: 4, z: 8 (z_hi: 2, z_lo: 4; z = z_hi * 4 + z_lo), core: 2. Of those that a mesh axis runs over, the one named last changes fastest.
Arguments:
- child_front: float32 [8, 12, 8, 2, 8, 12, 4, 128], P('cube', None, 'row', None, None, None, 'col'), may hold values from -6 to 25, as said below
- parent_front: float32 [12, 8, 8, 8, 12, 4, 128], P(None, 'row', 'cube', None, None, 'col'), may hold values from -6 to 25, as said below
- border_map: int32 [2, 11], replicated, may hold values from 0 to 11, as said below
Outputs:
- child_factor: float32 [8, 12, 8, 2, 8, 1, 4, 128], P('cube', None, 'row', None, None, None, 'col')
- parent_factor: float32 [12, 8, 8, 8, 1, 4, 128], P(None, 'row', 'cube', None, None, 'col')
- parent_update: float32 [11, 8, 8, 8, 11, 4, 128], P(None, 'row', 'cube', None, None, 'col')
Inputs may be any that keep to these rules, and one draw needn't show every extreme that they name: `child_front`: each C_c, read through the stated layout, is symmetric positive definite. `parent_front`: read as a matrix in natural order, the parent front is symmetric positive definite. `border_map`: each row lists 11 different parent blocks in increasing order.
All inputs are finite; a program needn't handle non-finite values.
Results may differ from a plain program's by a relative error of at most 0.00011.
Values sent between devices are 32-bit elements; how exact they have to be, the bound alone decides.
A program may use at most 64 MiB of HBM per device.

v0:
```python
import jax
import jax.numpy as jnp
from jax import lax
from jax.sharding import PartitionSpec as P

CHILD_PANELS = 1
PARENT_PANELS = 1
CHILDREN = 2


HIGHEST = lax.Precision.HIGHEST


def partner(block, axis, bit):
    count = lax.axis_size(axis)
    route = []
    for low in range(count):
        high = low | 1 << bit
        if high != low and high < count:
            route += [(low, high), (high, low)]
    return lax.ppermute(block, axis, route)


def lower_inverse(diagonal):
    lower = jnp.linalg.cholesky(diagonal)
    identity = jnp.eye(diagonal.shape[0], dtype=diagonal.dtype)
    return jax.scipy.linalg.solve_triangular(lower, identity, lower=True)


def own_columns(factor, col_block, start_rows):
    mine = lax.dynamic_slice_in_dim(factor, lax.axis_index("col") * col_block, col_block, 1)
    return jnp.concatenate([jnp.zeros((start_rows, col_block), factor.dtype), mine], 0)


def shards(child_front, parent_front, border_map):
    n_row = lax.axis_size("row")
    n_col = lax.axis_size("col")
    n_cube = lax.axis_size("cube")
    half = n_cube // CHILDREN
    child = lax.axis_index("cube") // half
    child_cycles = child_front.shape[1]
    sub_rows = child_front.shape[4]
    col_block = child_front.shape[7]
    block_rows = CHILDREN * sub_rows
    width = col_block * n_col
    natural_shape = (n_row, CHILDREN, half, sub_rows)
    front = child_front.reshape(child_cycles * block_rows, child_cycles * col_block)
    panel = 0
    row_start = panel * block_rows
    row_end = row_start + block_rows
    col_start = panel * col_block
    col_end = col_start + col_block
    top = front[row_start:row_end, col_start:]
    span = top.shape[1]
    piece = top[None]
    for bit in range(half.bit_length() - 1):
        other = partner(piece, "cube", bit)
        upper = lax.axis_index("cube") // 2**bit % 2 == 1
        piece = jnp.where(
            upper, jnp.concatenate([other, piece], 0), jnp.concatenate([piece, other], 0)
        )
    rows_whole = lax.all_gather(piece[None], "row", axis=0, tiled=True).reshape(width, span)
    gathered_shape = (n_row, half, CHILDREN, sub_rows)
    to_natural = (0, 2, 1, 3)
    to_gathered = (0, 2, 1, 3)
    corner_rows = rows_whole[:, :col_block].reshape(gathered_shape + (col_block,))
    corner_rows = corner_rows.transpose(to_natural + (4,)).reshape(width, col_block)
    corner = lax.all_gather(corner_rows, "col", axis=1, tiled=True)
    cols_whole = lax.all_gather(front[row_start:, col_start:col_end], "col", axis=1, tiled=True)
    inverse = lower_inverse(corner)
    mixing = (
        inverse.reshape((width,) + natural_shape)
        .transpose((0,) + tuple((1 + k for k in to_gathered)))
        .reshape(width, width)
    )
    factor = jnp.dot(cols_whole, inverse.T, precision=HIGHEST)
    across = jnp.dot(mixing, rows_whole, precision=HIGHEST)
    front = front.at[row_end:, col_end:].add(
        -jnp.dot(factor[block_rows:], across[:, col_block:], precision=HIGHEST)
    )
    child_columns = own_columns(factor, col_block, row_start)
    child_factor = child_columns.reshape(
        1, child_cycles, 1, CHILDREN, sub_rows, CHILD_PANELS, 1, col_block
    )
    parent_cycles = parent_front.shape[0]
    border_cycles = child_cycles - CHILD_PANELS
    border = front[CHILD_PANELS * block_rows :, CHILD_PANELS * col_block :]
    blocks = border.reshape(border_cycles, CHILDREN, sub_rows, border_cycles, col_block)
    kept = lax.dynamic_index_in_dim(blocks, child, 1, keepdims=False)
    sent = lax.dynamic_index_in_dim(blocks, 1 - child, 1, keepdims=False)
    received = partner(sent, "cube", half.bit_length() - 1)
    own_map = lax.dynamic_index_in_dim(border_map, child, 0, keepdims=False)
    sibling_map = lax.dynamic_index_in_dim(border_map, 1 - child, 0, keepdims=False)
    targets = jnp.arange(parent_cycles, dtype=jnp.int32)
    select = (jnp.stack([own_map, sibling_map], 0)[:, :, None] == targets[None, None, :]).astype(
        jnp.float32
    )
    contributions = jnp.stack([kept, received], 0)
    placed = jnp.einsum("cip,ciajb,cjq->paqb", select, contributions, select, precision=HIGHEST)
    assembled = parent_front.reshape(parent_cycles * sub_rows, parent_cycles * col_block)
    assembled = assembled + placed.reshape(parent_cycles * sub_rows, parent_cycles * col_block)
    panel = 0
    row_start = panel * sub_rows
    row_end = row_start + sub_rows
    col_start = panel * col_block
    col_end = col_start + col_block
    corner = assembled[row_start:row_end, col_start:col_end]
    pieces = lax.all_gather(corner[None], ("cube", "row", "col"), axis=0, tiled=True)
    diagonal = (
        pieces.reshape(n_cube, n_row, n_col, sub_rows, col_block)
        .transpose(1, 0, 3, 2, 4)
        .reshape(width, width)
    )
    inverse = lower_inverse(diagonal)
    top = assembled[row_start:row_end, col_start:]
    partial_rows = lax.all_gather(top[None, None], "cube", axis=1, tiled=True)
    sectioned = lax.all_gather(partial_rows, "row", axis=0, tiled=True)
    rows_whole = sectioned.reshape(width, top.shape[1])
    cols_whole = lax.all_gather(assembled[row_start:, col_start:col_end], "col", axis=1, tiled=True)
    factor = jnp.dot(cols_whole, inverse.T, precision=HIGHEST)
    across = jnp.dot(inverse, rows_whole, precision=HIGHEST)
    assembled = assembled.at[row_end:, col_end:].add(
        -jnp.dot(factor[sub_rows:], across[:, col_block:], precision=HIGHEST)
    )
    parent_columns = own_columns(factor, col_block, row_start)
    parent_factor = parent_columns.reshape(
        parent_cycles, 1, 1, sub_rows, PARENT_PANELS, 1, col_block
    )
    tail_cycles = parent_cycles - PARENT_PANELS
    tail = assembled[PARENT_PANELS * sub_rows :, PARENT_PANELS * col_block :]
    parent_update = tail.reshape(tail_cycles, 1, 1, sub_rows, tail_cycles, 1, col_block)
    return (child_factor, parent_factor, parent_update)


def solution(mesh):
    return jax.shard_map(
        shards,
        mesh=mesh,
        in_specs=(
            P("cube", None, "row", None, None, None, "col", None),
            P(None, "row", "cube", None, None, "col", None),
            P(),
        ),
        out_specs=(
            P("cube", None, "row", None, None, None, "col", None),
            P(None, "row", "cube", None, None, "col", None),
            P(None, "row", "cube", None, None, "col", None),
        ),
        check_vma=False,
    )
```

profile of v0, /device:TPU:1, one launch (start us, length us, event | category | flops | bytes accessed | tf_op | source)
XLA Modules:
  0.0 1031.7 jit_solution(7942101808400621147)
XLA Ops:
  8.5 3.3 collective-permute-start
  12.9 6.1 collective-permute-done.1
  19.8 92.6 %all-gather.7.cloned.1.call-done = f32[8,4,16,1536]{3,2,1,0:T(8,128)} async-done(((f32[1,4,16,1536]{3,2,1,0:T(8,128)}), f32[8,4,16,1536]{3,2,1,0:T(8,128)}) %all-gather.7.cloned.1.call-update) | async-done | bytes 3145744 | tf_op jit(solution)/shard_map/all_gather | solution.py:62
  114.3 2.9 reduce.21
  117.9 13.1 %all_gather.23 = f32[192,512]{1,0:T(8,128)} all-gather(f32[192,128]{1,0:T(8,128)S(1)} %slice.191), channel_id=1, replica_groups=mesh['cube'=8,'row'=8,'col'=4] {'col'}, dimensions={1}, use_global_device_ids=true | all-gather | bytes 491520 | tf_op jit(solution)/shard_map/all_gather | solution.py:69
  131.0 5.8 all-gather.9.cloned.1.call-done
  140.8 11.7 %cholesky.286 = f32[128,128]{1,0:T(8,128)S(1)} custom-call(f32[128,128]{1,0:T(8,128)S(1)} %cholesky.426), custom_call_target="Cholesky" | custom-call | tf_op jit(solution)/shard_map/jit(cholesky)/cholesky | solution.py:25
  152.7 9.8 custom-call.27
  165.6 12.5 %cholesky.305 = f32[128,128]{1,0:T(8,128)S(1)} custom-call(f32[128,128]{1,0:T(8,128)} %cholesky.430), custom_call_target="Cholesky" | custom-call | tf_op jit(solution)/shard_map/jit(cholesky)/cholesky | solution.py:25
  178.8 11.0 %custom-call.28 = f32[1,128,128]{1,2,0:T(8,128)S(1)} custom-call(f32[1,128,128]{2,1,0:T(8,128)} %get-tuple-element.95), custom_call_target="InvertDiagBlocksLowerTriangular" | custom-call | tf_op jit(solution)/shard_map/jit(cholesky)/cholesky | solution.py:25
  191.4 11.7 %cholesky.326 = f32[128,128]{1,0:T(8,128)S(1)} custom-call(f32[128,128]{1,0:T(8,128)S(1)} %cholesky.435), custom_call_target="Cholesky" | custom-call | tf_op jit(solution)/shard_map/jit(cholesky)/cholesky | solution.py:25
  203.8 9.8 custom-call.29
  215.1 11.7 %cholesky.343 = f32[128,128]{1,0:T(8,128)S(1)} custom-call(f32[128,128]{1,0:T(8,128)S(1)} %convolution_subtract_fusion.11), custom_call_target="Cholesky" | custom-call | tf_op jit(solution)/shard_map/jit(cholesky)/cholesky | solution.py:25
  231.9 11.6 %while.6 = (s32[]{:T(128)}, f32[512,512]{1,0:T(8,128)}, s32[4,2]{0,1:T(2,128)S(1)}, f32[4,128,128]{2,1,0:T(8,128)S(1)}, s32[]{:T(128)}) while((s32[]{:T(128)}, f32[512,512]{1,0:T(8,128)}, s32[4,2]{0,1:T(2,128)S(1)}, f32[4,128,128]{2,1,0:T(8,128)S(1)}, s32[]{:T(128)}) %tuple.69), condition=%wide.while_cond.2, body=%wide.while_body.2.sunk | while | flops 2 | bytes 131181 | solution.py:27
  243.5 39.3 %custom-call.30 = f32[4,128,128]{1,2,0:T(8,128)S(1)} custom-call(f32[4,128,128]{2,1,0:T(8,128)S(1)} %get-tuple-element.43), custom_call_target="InvertDiagBlocksLowerTriangular" | custom-call | tf_op jit(solution)/shard_map/jit(_solve_triangular)/triangular_solve | solution.py:27
  290.6 2.5 copy.37
  294.4 7.3 fusion.2
  305.2 3.1 collective-permute-start.2
  310.9 19.0 %collective-permute-done.2 = f32[11,8,11,128]{3,1,2,0:T(8,128)} collective-permute-done((f32[11,8,11,128]{3,1,2,0:T(8,128)S(1)}, f32[11,8,11,128]{3,1,2,0:T(8,128)}, u32[]{:S(2)}, u32[]{:S(2)}) %collective-permute-start.2) | collective-permute-done | bytes 495648 | tf_op jit(solution)/shard_map/ppermute | solution.py:21
  335.9 10.1 all_gather.24
  346.0 19.6 %all-gather.1 = f32[64,1536]{1,0:T(8,128)} all-gather(f32[8,1536]{1,0:T(8,128)S(1)} %slice.199), channel_id=3, replica_groups=mesh['cube'=8,'row'=8,'col'=4] {'cube'}, dimensions={0}, use_global_device_ids=true | all-gather | bytes 442368 | tf_op jit(solution)/shard_map/all_gather | solution.py:116
  365.6 506.2 %all-gather.13.cloned.1.call-done = f32[2048,128]{1,0:T(8,128)} async-done(((f32[8,128]{1,0:T(8,128)}), f32[2048,128]{1,0:T(8,128)}) %all-gather.13.cloned.1.call-update) | async-done | bytes 1048592 | tf_op jit(solution)/shard_map/all_gather | solution.py:108
  874.8 11.7 %cholesky.358 = f32[128,128]{1,0:T(8,128)S(1)} custom-call(f32[128,128]{1,0:T(8,128)S(1)} %cholesky.439), custom_call_target="Cholesky" | custom-call | tf_op jit(solution)/shard_map/jit(cholesky)/cholesky | solution.py:25
  886.6 9.8 custom-call.31
  899.0 11.7 %cholesky.377 = f32[128,128]{1,0:T(8,128)S(1)} custom-call(f32[128,128]{1,0:T(8,128)S(1)} %cholesky.443), custom_call_target="Cholesky" | custom-call | tf_op jit(solution)/shard_map/jit(cholesky)/cholesky | solution.py:25
  910.7 9.9 custom-call.32
  922.2 11.7 %cholesky.398 = f32[128,128]{1,0:T(8,128)S(1)} custom-call(f32[128,128]{1,0:T(8,128)S(1)} %cholesky.448), custom_call_target="Cholesky" | custom-call | tf_op jit(solution)/shard_map/jit(cholesky)/cholesky | solution.py:25
  934.0 9.8 custom-call.33
  945.3 11.9 %cholesky.415 = f32[128,128]{1,0:T(8,128)S(1)} custom-call(f32[128,128]{1,0:T(8,128)S(1)} %convolution_subtract_fusion.10), custom_call_target="Cholesky" | custom-call | tf_op jit(solution)/shard_map/jit(cholesky)/cholesky | solution.py:25
  962.5 8.0 while.7
  970.5 39.3 %custom-call.34 = f32[4,128,128]{1,2,0:T(8,128)S(1)} custom-call(f32[4,128,128]{2,1,0:T(8,128)S(1)} %get-tuple-element.44), custom_call_target="InvertDiagBlocksLowerTriangular" | custom-call | tf_op jit(solution)/shard_map/jit(_solve_triangular)/triangular_solve | solution.py:27
  1014.8 7.2 fusion
  (147 shorter events, 79.4 us)
Async XLA Ops:
  7.2 107.2 %copy-start.4 = (f32[1,12,1,2,8,12,1,128]{7,6,5,4,3,2,1,0:T(1,128)S(1)}, f32[1,12,1,2,8,12,1,128]{7,6,5,4,3,2,1,0:T(1,128)}, u32[]{:S(2)}) copy-start(f32[1,12,1,2,8,12,1,128]{7,6,5,4,3,2,1,0:T(1,128)} %param.10) | copy-start | bytes 3538948
  7.2 105.2 %all-gather.7.cloned.1.call-start = ((), (), s32[]{:S(2)}) async-start(), calls=%async_computation | async-start | bytes 3538944 | tf_op jit(solution)/shard_map/all_gather | solution.py:62
  8.5 4.2 collective-permute-start
  12.7 6.2 collective-permute-start.1
  19.7 117.1 %all-gather.9.cloned.1.call-start = ((), (), s32[]{:S(2)}) async-start(), calls=%async_computation.1 | async-start | bytes 1310720 | tf_op jit(solution)/shard_map/all_gather | solution.py:68
  114.3 757.6 %all-gather.13.cloned.1.call-start = ((), (), s32[]{:S(2)}) async-start(), calls=%async_computation.3 | async-start | bytes 1052672 | tf_op jit(solution)/shard_map/all_gather | solution.py:108
  139.8 1.0 copy-start
  282.8 3.8 copy-start.7
  294.4 7.3 copy-start.6
  303.0 2.2 copy-start.5
  305.1 5.7 copy-start.9
  305.2 24.7 %collective-permute-start.2 = (f32[11,8,11,128]{3,1,2,0:T(8,128)S(1)}, f32[11,8,11,128]{3,1,2,0:T(8,128)}, u32[]{:S(2)}, u32[]{:S(2)}) collective-permute-start(f32[11,8,11,128]{3,1,2,0:T(8,128)S(1)} %get-tuple-element.78), channel_id=1, source_target_pairs={{0,128},{128,0},{32,160},{160,32},{64,192},{192,64},{96,224},{224,... | collective-permute-start | bytes 1486856 | tf_op jit(solution)/shard_map/ppermute | solution.py:21
  333.6 539.6 %copy-start.2 = (f32[96,1536]{1,0:T(8,128)}, f32[96,1536]{1,0:T(8,128)S(1)}, u32[]{:S(2)}) copy-start(f32[96,1536]{1,0:T(8,128)S(1)} %bitcast_add_fusion.2) | copy-start | bytes 1769476
  334.3 680.4 %all-gather.11.cloned.1.call-start = ((), (), s32[]{:S(2)}) async-start(), calls=%async_computation.2 | async-start | bytes 3538944 | tf_op jit(solution)/shard_map/all_gather | solution.py:117
  873.8 1.0 copy-start.1
  1009.8 3.2 copy-start.8
  1014.8 7.2 copy-start.3
Sparse Core Ops, SparseCore 0:
  19.8 92.5 all-gather.6
  114.8 21.9 all-gather.8
  334.4 537.3 all-gather.12
  874.3 87.2 all-gather.10
where the time goes:
time: 1040 us; the launch traced here: 1030 us
  waiting for transfers between devices  631 us (61%)
  other arithmetic  250 us (24%)
  matrix products  43.2 us (4%)
  blocking collectives  42.8 us (4%)
  local copies, waits for them, and re-layouts  38.4 us (4%)
  between operations  19.9 us (2%)
    all_gather x1, waiting for transfers between devices, shards(): lax.all_gather(corner[None], ('cube', 'row', 'col'), axis=0, tiled=True)  506 us
    another operation x29, other arithmetic, lower_inverse(): lower = jnp.linalg.cholesky(diagonal)  160 us
    all_gather x1, waiting for transfers between devices, shards(): lax.all_gather(piece[None], 'row', axis=0, tiled=True).reshape(width, span)  92.6 us
    another operation x6, other arithmetic, lower_inverse(): return jax.scipy.linalg.solve_triangular(lower, identity, lower=True)  80.9 us
    ppermute x3, waiting for transfers between devices, partner(): return lax.ppermute(block, axis, route)  26 us
    another operation x28, local copies, waits for them, and re-layouts, lower_inverse(): return jax.scipy.linalg.solve_triangular(lower, identity, lower=True)  22 us
  transfers between devices with their start and end apart: 7, of which 6 were waited for; matrix products, arithmetic and copies ran while one was open for 14% of the time, Pallas kernels for 0%

commit v1 on v0

--- a/solution.py
+++ b/solution.py
@@ -1,6 +1,10 @@
+import functools
+
 import jax
 import jax.numpy as jnp
 from jax import lax
+from jax.experimental import pallas as pl
+from jax.experimental.pallas import tpu as pltpu
 from jax.sharding import PartitionSpec as P
 
 CHILD_PANELS = 1
@@ -9,6 +13,76 @@
 
 
 HIGHEST = lax.Precision.HIGHEST
+HI = HIGHEST
+NB=128
+
+def base(T, out_ref, w):
+    rows = list(T)
+    lane = lax.broadcasted_iota(jnp.int32, (8, NB), 1)
+    sub = lax.broadcasted_iota(jnp.int32, (8, NB), 0)
+    n = NB // 8
+    bc_lane = lambda x, j: jnp.broadcast_to(x[:, j:j+1], (8, NB))
+    bc_sub = lambda x, s: jnp.broadcast_to(x[s:s+1, :], (8, NB))
+    for j in range(0, NB, w):
+        t, s = j // 8, j % 8
+        c = [{i: bc_lane(rows[i], j + a) for i in range(t, n)} for a in range(w)]
+        inblk = (lane >= j) & (lane < j + w)
+        r = []
+        for a in range(w):
+            x = bc_sub(rows[t], s + a)
+            x = jnp.where(lane == j + a, 1.0, jnp.where(inblk, 0.0, x) if w > 1 else x)
+            r.append(x)
+        pv = {(a, b): bc_sub(c[b][t], s + a) for a in range(w) for b in range(a, w)}
+        z = []
+        for a in range(w):
+            inv = 1.0 / pv[a, a]
+            rs = lax.rsqrt(pv[a, a])
+            za = r[a] * inv
+            z.append(za)
+            row = jnp.where(lane <= j + a, r[a] * rs, 0.0)
+            out_ref[j + a:j + a + 1, :] = row[:1, :]
+            for b in range(a + 1, w):
+                m = pv[a, b] * inv
+                r[b] = r[b] - pv[a, b] * za
+                for d in range(b, w):
+                    pv[b, d] = pv[b, d] - m * pv[a, d]
+                for i in range(t, n):
+                    c[b][i] = c[b][i] - c[a][i] * m
+        for i in range(t, n):
+            if i == t and s + w == 8:
+                continue
+            acc = jnp.where(inblk, 0.0, rows[i])
+            for a in range(w):
+                acc = acc - c[a][i] * z[a]
+            rows[i] = acc if i > t else jnp.where(sub >= s + w, acc, rows[i])
+
+def chol_inv(B, Vd, w, n=512):
+    nk = n // NB
+    for k in range(nk):
+        kb = slice(k*NB, (k+1)*NB)
+        T = [B[k*NB+8*i:k*NB+8*i+8, kb] for i in range(NB//8)]
+        base(T, Vd, w)
+        V = Vd[...]
+        if k + 1 < nk:
+            rest = slice((k+1)*NB, n)
+            L = lax.dot_general(B[rest, kb], V, (((1,), (1,)), ((), ())), precision=HI, preferred_element_type=jnp.float32)
+            R2 = jnp.dot(V, B[kb, rest], precision=HI, preferred_element_type=jnp.float32)
+        if k:
+            left = slice(0, k*NB)
+            R1 = jnp.dot(V, B[kb, left], precision=HI, preferred_element_type=jnp.float32)
+            B[kb, left] = R1
+        B[kb, kb] = V
+        if k + 1 < nk:
+            if k:
+                B[rest, left] = B[rest, left] - jnp.dot(L, R1, precision=HI, preferred_element_type=jnp.float32)
+            B[rest, kb] = -jnp.dot(L, V, precision=HI, preferred_element_type=jnp.float32)
+            B[rest, rest] = B[rest, rest] - jnp.dot(L, R2, precision=HI, preferred_element_type=jnp.float32)
+            B[kb, rest] = jnp.zeros((NB, n-(k+1)*NB), jnp.float32)
+
+def kern(w, a, o, B, Vd):
+    B[...] = a[...]
+    chol_inv(B, Vd, w)
+    o[...] = B[...]
 
 
 def partner(block, axis, bit):
@@ -22,9 +96,14 @@
 
 
 def lower_inverse(diagonal):
-    lower = jnp.linalg.cholesky(diagonal)
-    identity = jnp.eye(diagonal.shape[0], dtype=diagonal.dtype)
-    return jax.scipy.linalg.solve_triangular(lower, identity, lower=True)
+    return pl.pallas_call(
+        functools.partial(kern, 8),
+        out_shape=jax.ShapeDtypeStruct(diagonal.shape, jnp.float32),
+        in_specs=[pl.BlockSpec(memory_space=pltpu.VMEM)],
+        out_specs=pl.BlockSpec(memory_space=pltpu.VMEM),
+        scratch_shapes=[pltpu.VMEM(diagonal.shape, jnp.float32), pltpu.VMEM((NB, NB), jnp.float32)],
+        name="inverse_factor",
+    )(diagonal)
 
 
 def own_columns(factor, col_block, start_rows):

time: 1040 us -> 853 us (0.82)
  other arithmetic: 250 us -> 5.7 us
  waiting for transfers between devices: 631 us -> 700 us
  Pallas kernels: 0 us -> 49.8 us
  local copies, waits for them, and re-layouts: 38.4 us -> 10.9 us
  matrix products: 43.2 us -> 24.3 us
    another operation x35 -> x0, other arithmetic: 241 us -> none  [the longest x29 160 us: lower_inverse(): lower = jnp.linalg.cholesky(diagonal)]
    all_gather x1, waiting for transfers between devices: 0.01 us -> 59.1 us  [shards(): sectioned = lax.all_gather(partial_rows, 'row', axis=0, tiled=True)]
    pallas_call x0 -> x2, Pallas kernels: none -> 49.8 us  [lower_inverse(): pl.pallas_call(functools.partial(kern, 8), out_shape=jax.ShapeDtypeStruct...]
    another operation x37 -> x1, local copies, waits for them, and re-layouts: 24.4 us -> 0.66 us  [the longest x28 22 us: lower_inverse(): return jax.scipy.linalg.solve_triangular(lower, identity, lower=True)]
    another operation x26 -> x0, matrix products: 20.6 us -> none  [the longest x12 10.9 us: lower_inverse(): lower = jnp.linalg.cholesky(diagonal)]
  transfers between devices with their start and end apart: 7 -> 7, of which waited for: 6 -> 7; matrix products, arithmetic and copies ran while one was open for 14% -> 1% of each run, Pallas kernels for 0% -> 3%
where the time goes in v1:
time: 853 us; the launch traced here: 848 us
  waiting for transfers between devices  700 us (82%)
  Pallas kernels  49.8 us (6%)
  blocking collectives  38.3 us (4%)
  matrix products  24.3 us (3%)
  between operations  14.4 us (2%)
  local copies, waits for them, and re-layouts  10.9 us (1%)
    all_gather x1, waiting for transfers between devices, shards(): lax.all_gather(corner[None], ('cube', 'row', 'col'), axis=0, tiled=True)  511 us
    all_gather x1, waiting for transfers between devices, shards(): lax.all_gather(piece[None], 'row', axis=0, tiled=True).reshape(width, span)  92.6 us
    all_gather x1, waiting for transfers between devices, shards(): sectioned = lax.all_gather(partial_rows, 'row', axis=0, tiled=True)  59.1 us
    pallas_call x2, Pallas kernels, lower_inverse(): pl.pallas_call(functools.partial(kern, 8), out_shape=jax.ShapeDtypeStruct...  49.8 us
    ppermute x3, waiting for transfers between devices, partner(): return lax.ppermute(block, axis, route)  27.3 us
    all_gather x1, blocking collectives, shards(): partial_rows = lax.all_gather(top[None, None], 'cube', axis=1, tiled=True)  17.5 us
  transfers between devices with their start and end apart: 7, of which 7 were waited for; matrix products, arithmetic and copies ran while one was open for 1% of the time, Pallas kernels for 3%

profile of v1, /device:TPU:1, one launch (start us, length us, event | category | flops | bytes accessed | tf_op | source)
XLA Modules:
  0.0 848.2 jit_solution(6737605436543032587)
XLA Ops:
  7.2 1.2 slice_reduce_fusion
  8.5 3.3 collective-permute-start
  11.8 0.9 collective-permute-done
  12.9 6.1 collective-permute-done.1
  18.9 0.8 maximum_select_fusion
  19.8 92.6 %all-gather.7.cloned.1.call-done = f32[8,4,16,1536]{3,2,1,0:T(8,128)} async-done(((f32[1,4,16,1536]{3,2,1,0:T(8,128)}), f32[8,4,16,1536]{3,2,1,0:T(8,128)}) %all-gather.7.cloned.1.call-update) | async-done | bytes 3145744 | tf_op jit(solution)/shard_map/all_gather | solution.py:141
  112.4 1.0 slice.97
  113.4 0.7 copy.26
  114.2 2.9 reduce.5
  117.6 11.5 %all_gather.23 = f32[192,512]{1,0:T(8,128)S(1)} all-gather(f32[192,128]{1,0:T(8,128)S(1)} %slice.98), channel_id=1, replica_groups=mesh['cube'=8,'row'=8,'col'=4] {'col'}, dimensions={1}, use_global_device_ids=true | all-gather | bytes 491520 | tf_op jit(solution)/shard_map/all_gather | solution.py:148
  129.1 9.9 %all-gather.9.cloned.1.call-done.a = f32[512,512]{1,0:T(8,128)} async-done(((f32[512,128]{1,0:T(8,128)}), f32[512,512]{1,0:T(8,128)}) %all-gather.9.cloned.1.call-update) | async-done | bytes 1048592 | tf_op jit(solution)/shard_map/all_gather | solution.py:147
  139.0 25.1 %inverse_factor.2 = f32[512,512]{1,0:T(8,128)} custom-call(f32[512,512]{1,0:T(8,128)} %all-gather.9.cloned.1.call-done.a), custom_call_target="tpu_custom_call" | custom-call | tf_op jit(solution)/shard_map/inverse_factor/pallas_call | solution.py:99
  164.0 1.6 copy.27
  165.7 7.3 fusion.2
  173.0 1.2 fusion.25
  174.3 2.2 fusion.4
  176.6 1.3 collective-permute-start.2
  177.9 1.4 reduce.6
  179.5 20.2 %collective-permute-done.2 = f32[11,8,11,128]{3,1,2,0:T(8,128)S(1)} collective-permute-done((f32[11,8,11,128]{3,1,2,0:T(8,128)S(1)}, f32[11,8,11,128]{3,1,2,0:T(8,128)S(1)}, u32[]{:S(2)}, u32[]{:S(2)}) %collective-permute-start.2) | collective-permute-done | bytes 495648 | tf_op jit(solution)/shard_map/ppermute | solution.py:95
  199.9 0.9 fusion.8
  200.8 1.1 fusion.12
  203.2 17.5 %all-gather.1 = f32[64,1536]{1,0:T(8,128)} all-gather(f32[8,1536]{1,0:T(8,128)S(1)} %slice.106), channel_id=3, replica_groups=mesh['cube'=8,'row'=8,'col'=4] {'cube'}, dimensions={0}, use_global_device_ids=true | all-gather | bytes 442368 | tf_op jit(solution)/shard_map/all_gather | solution.py:195
  220.7 0.7 constant_dynamic-slice_fusion.4
  221.4 9.2 %all_gather.24 = f32[96,512]{1,0:T(8,128)S(1)} all-gather(f32[96,128]{1,0:T(8,128)S(1)} %slice.102), channel_id=1, replica_groups=mesh['cube'=8,'row'=8,'col'=4] {'col'}, dimensions={1}, use_global_device_ids=true | all-gather | bytes 245760 | tf_op jit(solution)/shard_map/all_gather | solution.py:198
  230.6 511.0 %all-gather.13.cloned.1.call-done = f32[2048,128]{1,0:T(8,128)} async-done(((f32[8,128]{1,0:T(8,128)}), f32[2048,128]{1,0:T(8,128)}) %all-gather.13.cloned.1.call-update) | async-done | bytes 1048592 | tf_op jit(solution)/shard_map/all_gather | solution.py:187
  741.6 2.3 copy.33
  743.9 24.8 %inverse_factor.3 = f32[512,512]{1,0:T(8,128)} custom-call(f32[512,512]{1,0:T(8,128)} %bitcast.72), custom_call_target="tpu_custom_call" | custom-call | tf_op jit(solution)/shard_map/inverse_factor/pallas_call | solution.py:99
  768.7 2.4 fusion.26
  771.7 59.1 %all-gather.11.cloned.1.call-done = f32[8,8,8,1536]{3,2,1,0:T(8,128)} async-done(((f32[1,8,8,1536]{3,2,1,0:T(8,128)}), f32[8,8,8,1536]{3,2,1,0:T(8,128)}) %all-gather.11.cloned.1.call-update) | async-done | bytes 3145744 | tf_op jit(solution)/shard_map/all_gather | solution.py:196
  830.8 7.5 fusion
  838.3 1.6 fusion.15
  840.0 1.3 copy.35
  (33 shorter events, 3.1 us)
Async XLA Ops:
  7.2 107.0 %copy-start.1 = (f32[1,12,1,2,8,12,1,128]{7,6,5,4,3,2,1,0:T(1,128)S(1)}, f32[1,12,1,2,8,12,1,128]{7,6,5,4,3,2,1,0:T(1,128)}, u32[]{:S(2)}) copy-start(f32[1,12,1,2,8,12,1,128]{7,6,5,4,3,2,1,0:T(1,128)} %param.7) | copy-start | bytes 3538948
  7.2 105.2 %all-gather.7.cloned.1.call-start = ((), (), s32[]{:S(2)}) async-start(), calls=%async_computation | async-start | bytes 3538944 | tf_op jit(solution)/shard_map/all_gather | solution.py:141
  8.5 4.2 collective-permute-start
  12.7 6.2 collective-permute-start.1
  19.7 119.3 %all-gather.9.cloned.1.call-start = ((), (), s32[]{:S(2)}) async-start(), calls=%async_computation.1 | async-start | bytes 1310720 | tf_op jit(solution)/shard_map/all_gather | solution.py:147
  114.1 627.5 %all-gather.13.cloned.1.call-start = ((), (), s32[]{:S(2)}) async-start(), calls=%async_computation.3 | async-start | bytes 1052672 | tf_op jit(solution)/shard_map/all_gather | solution.py:187
  165.7 7.4 copy-start
  174.3 3.6 copy-start.2
  176.5 2.8 copy-start.3
  176.6 23.1 %collective-permute-start.2 = (f32[11,8,11,128]{3,1,2,0:T(8,128)S(1)}, f32[11,8,11,128]{3,1,2,0:T(8,128)S(1)}, u32[]{:S(2)}, u32[]{:S(2)}) collective-permute-start(f32[11,8,11,128]{3,1,2,0:T(8,128)S(1)} %get-tuple-element.40), channel_id=1, source_target_pairs={{0,128},{128,0},{32,160},{160,32},{64,192},{192,64},{96,224},{224,... | collective-permute-start | bytes 1486856 | tf_op jit(solution)/shard_map/ppermute | solution.py:95
  203.1 627.7 %all-gather.11.cloned.1.call-start = ((), (), s32[]{:S(2)}) async-start(), calls=%async_computation.2 | async-start | bytes 3538944 | tf_op jit(solution)/shard_map/all_gather | solution.py:196
Sparse Core Ops, SparseCore 0:
  19.8 92.5 all-gather.6
  114.8 24.1 all-gather.8
  203.2 538.3 all-gather.12
  744.1 86.6 all-gather.10

commit v2 on v0

v2 whole, which is shorter than its diff:
```python
import functools

import jax
import jax.numpy as jnp
from jax import lax
from jax.experimental import pallas as pl
from jax.experimental.pallas import tpu as pltpu
from jax.sharding import PartitionSpec as P

CHILDREN = 2
SUB = 8
LANE = 128
WIDTH = 512
STEP = 8
HIGHEST = lax.Precision.HIGHEST
MESH = pl.DeviceIdType.MESH
F32 = jnp.float32


def mm(a, b):
    return jnp.dot(a, b, precision=HIGHEST, preferred_element_type=F32)


def mm_t(a, b):
    return lax.dot_general(
        a, b, (((1,), (1,)), ((), ())), precision=HIGHEST, preferred_element_type=F32
    )


def diagonal_inverse(tiles, out_ref):
    rows = list(tiles)
    lane = lax.broadcasted_iota(jnp.int32, (SUB, LANE), 1)
    n = LANE // SUB
    for t in range(n):
        j = t * SUB
        column = [
            {i: jnp.broadcast_to(rows[i][:, j + a : j + a + 1], (SUB, LANE)) for i in range(t, n)}
            for a in range(STEP)
        ]
        inside = (lane >= j) & (lane < j + STEP)
        right = []
        for a in range(STEP):
            row = jnp.broadcast_to(rows[t][a : a + 1, :], (SUB, LANE))
            right.append(jnp.where(lane == j + a, 1.0, jnp.where(inside, 0.0, row)))
        pivot = {
            (a, b): jnp.broadcast_to(column[b][t][a : a + 1, :], (SUB, LANE))
            for a in range(STEP)
            for b in range(a, STEP)
        }
        scaled = []
        for a in range(STEP):
            inverse = 1.0 / pivot[a, a]
            scaled.append(right[a] * inverse)
            row = jnp.where(lane <= j + a, right[a] * lax.rsqrt(pivot[a, a]), 0.0)
            out_ref[j + a : j + a + 1, :] = row[:1, :]
            for b in range(a + 1, STEP):
                ratio = pivot[a, b] * inverse
                right[b] = right[b] - pivot[a, b] * scaled[a]
                for d in range(b, STEP):
                    pivot[b, d] = pivot[b, d] - ratio * pivot[a, d]
                for i in range(t + 1, n):
                    column[b][i] = column[b][i] - column[a][i] * ratio
        for i in range(t + 1, n):
            rest = jnp.where(inside, 0.0, rows[i])
            for a in range(STEP):
                rest = rest - column[a][i] * scaled[a]
            rows[i] = rest


def inverse_factor(matrix, block, strip, hook):
    blocks = WIDTH // LANE

    def body(k, carry):
        here = pl.ds(pl.multiple_of(k * LANE, LANE), LANE)
        tiles = [
            matrix[pl.ds(pl.multiple_of(k * LANE + SUB * i, SUB), SUB), here]
            for i in range(LANE // SUB)
        ]
        diagonal_inverse(tiles, block)
        hook(k)
        strip[...] = mm(block[...], matrix[here, :])
        strip[:, here] = block[...]
        for i in range(1, blocks):
            below = slice(i * LANE, (i + 1) * LANE)

            @pl.when(k < i)
            def _():
                left = mm_t(matrix[below, here], block[...])
                matrix[below, here] = jnp.zeros((LANE, LANE), F32)
                matrix[below, :] = matrix[below, :] - mm(left, strip[...])

        for i in range(blocks):
            columns = slice(i * LANE, (i + 1) * LANE)
            matrix[here, columns] = jnp.where(k >= i, strip[:, columns], 0.0)
        return carry

    lax.fori_loop(0, blocks, body, 0)


def place():
    cube, row, col = lax.axis_index("cube"), lax.axis_index("row"), lax.axis_index("col")
    return cube, row, col


class Sends:
    def __init__(self, send, recv):
        self.send, self.recv, self.copies = send, recv, []

    def add(self, src, dst, device):
        index = len(self.copies)
        copy = pltpu.make_async_remote_copy(
            src_ref=src,
            dst_ref=dst,
            send_sem=self.send.at[index],
            recv_sem=self.recv.at[index],
            device_id=device,
            device_id_type=MESH,
        )
        self.copies.append(copy)

    def start(self):
        for copy in self.copies:
            copy.start()

    def arrived(self):
        for copy in self.copies:
            copy.wait_recv()

    def left(self):
        for copy in self.copies:
            copy.wait_send()


def greet(peers):
    barrier = pltpu.get_barrier_semaphore()
    for device in peers:
        pl.semaphore_signal(barrier, inc=1, device_id=device, device_id_type=MESH)
    pl.semaphore_wait(barrier, len(peers))


def child_kernel(
    front, factor, update,
    panel, corner, across, matrix, block, strip, wide, whole, local,
    s_y, r_y, s_rest, r_rest, s_dz, r_dz, s_dx, r_dx, s_dc, r_dc, s_az, r_az, s_ax, r_ax, s_ac, r_ac,
):
    cube, row, col = place()
    core, zl, child = cube % 2, cube // 2 % 2, cube // 4
    x, zh = row % 4, row // 4
    cycles = front.shape[0]
    ys = [(cube, row, (col + d) % 4) for d in (1, 2, 3)]
    zs = [
        (child * 4 + (zl + d % 2) % 2 * 2 + core, (zh + d // 2) % 2 * 4 + x, col) for d in (1, 2, 3)
    ]
    xs = [(cube, zh * 4 + (x + d) % 4, col) for d in (1, 2, 3)]
    other = (cube + 1 - 2 * core, row, col)
    greet(ys + zs + xs + [other])

    first, rest = Sends(s_y, r_y), Sends(s_rest, r_rest)
    for device in ys:
        first.add(front.at[0, :, :, 0:LANE], panel.at[col, 0], device)
    for device in ys:
        rest.add(front.at[1:, :, :, 0:LANE], panel.at[col, 1:], device)
    first.start()
    own = pltpu.make_async_copy(front.at[:, :, :, 0:LANE], panel.at[col], local.at[0])
    own.start()
    mine = pltpu.make_async_copy(
        front.at[0, :, :, LANE:], across.at[zh, x, :, zl, core], local.at[1]
    )
    mine.start()
    dz, dx, dc = Sends(s_dz, r_dz), Sends(s_dx, r_dx), Sends(s_dc, r_dc)
    az, ax, ac = Sends(s_az, r_az), Sends(s_ax, r_ax), Sends(s_ac, r_ac)
    own.wait()
    first.arrived()
    placed = pltpu.make_async_copy(
        panel.at[:, 0], corner.at[:, zh, x, :, zl, core], local.at[2]
    )
    placed.start()
    for device in zs:
        dz.add(panel.at[:, 0], corner.at[:, zh, x, :, zl, core], device)
    dz.start()
    rest.start()
    placed.wait()
    mine.wait()
    dz.arrived()
    for device in xs:
        for a in range(2):
            for b in range(2):
                piece = corner.at[:, a, x, :, b, core]
                dx.add(piece, piece, device)
    dx.start()
    for device in zs:
        az.add(front.at[0, :, :, LANE:], across.at[zh, x, :, zl, core], device)
    dx.arrived()
    for a in range(2):
        for b in range(4):
            for c in range(2):
                piece = corner.at[:, a, b, :, c, core]
                dc.add(piece, piece, other)
    dc.start()
    az.start()
    for device in xs:
        for a in range(2):
            for b in range(2):
                piece = across.at[a, x, :, b, core]
                ax.add(piece, piece, device)
    for a in range(2):
        for b in range(4):
            for c in range(2):
                piece = across.at[a, b, :, c, core]
                ac.add(piece, piece, other)
    dc.arrived()
    for i in range(4):
        matrix[:, i * LANE : (i + 1) * LANE] = corner[i].reshape(WIDTH, LANE)

    def hook(k):
        @pl.when(k == 0)
        def _():
            az.arrived()
            ax.start()

        @pl.when(k == 2)
        def _():
            ax.arrived()
            ac.start()

    inverse_factor(matrix, block, strip, hook)
    rest.arrived()
    for i in range(4):
        wide[:, i * LANE : (i + 1) * LANE] = panel[i].reshape(cycles * 2 * SUB, LANE)
    whole[...] = mm_t(wide[...], matrix[...])
    factor[...] = whole[:, pl.ds(pl.multiple_of(col * LANE, LANE), LANE)]
    wide[...] = mm(whole[...], matrix[...])
    ac.arrived()
    border = cycles - 1
    width = border * LANE
    for begin in range(0, width, 2 * LANE):
        size = min(2 * LANE, width - begin)
        product = mm(
            wide[2 * SUB :, :], across[:, :, :, :, :, :, begin : begin + size].reshape(WIDTH, size)
        ).reshape(border, 2, SUB, size)
        for h in range(2):
            update[h, :, :, begin : begin + size] = (
                front[1:, h, :, LANE + begin : LANE + begin + size] - product[:, h]
            )
    for stage in (first, rest, dz, dx, dc, az, ax, ac):
        stage.left()


def parent_kernel(
    border_map, update, front, factor, tail,
    taken, total, panel, corner, across, matrix, block, strip, wide, whole, local,
    s_p, r_p, s_y, r_y, s_rest, r_rest, s_dz, r_dz, s_dx, r_dx, s_dc, r_dc, s_az, r_az, s_ax, r_ax, s_ac, r_ac,
):
    cube, row, col = place()
    core, zl, child = cube % 2, cube // 2, cube // 4
    x, zh = row % 4, row // 4
    cycles = front.shape[0]
    border = cycles - 1
    partner = ((cube + 4) % 8, row, col)
    ys = [(cube, row, (col + d) % 4) for d in (1, 2, 3)]
    zs = [((zl + d % 4) % 4 * 2 + core, (zh + d // 4) % 2 * 4 + x, col) for d in range(1, 8)]
    xs = [(cube, zh * 4 + (x + d) % 4, col) for d in (1, 2, 3)]
    other = (cube + 1 - 2 * core, row, col)
    greet(ys + zs + xs + [other])

    sibling = Sends(s_p, r_p)
    sibling.add(update.at[1 - child, 0], taken.at[0], partner)
    sibling.add(update.at[1 - child, 1:, :, 0:LANE], taken.at[1:, :, 0:LANE], partner)
    sibling.add(update.at[1 - child, 1:, :, LANE:], taken.at[1:, :, LANE:], partner)
    sibling.start()

    skipped = []
    for index in (child, 1 - child):
        count = cycles * (cycles - 1) // 2
        for i in range(border):
            count = count - border_map[index, i]
        skipped.append(count)

    def shifted(pick, hole, p):
        before = pick(p) if p < border else None
        after = pick(p - 1) if p else None
        if before is None:
            return jnp.where(hole < p, after, 0.0)
        if after is None:
            return jnp.where(hole > p, before, 0.0)
        return jnp.where(hole > p, before, jnp.where(hole < p, after, 0.0))

    sources = (lambda i, j: update[child, i, :, j * LANE : (j + 1) * LANE],
               lambda i, j: taken[i, :, j * LANE : (j + 1) * LANE])

    def assemble(p, q):
        value = front[p, :, q * LANE : (q + 1) * LANE]
        for source, hole in zip(sources, skipped):
            value = value + shifted(
                lambda i: shifted(lambda j: source(i, j), hole, q), hole, p
            )
        total[p, :, q * LANE : (q + 1) * LANE] = value

    sibling.copies[0].wait_recv()
    assemble(0, 0)
    first, rest = Sends(s_y, r_y), Sends(s_rest, r_rest)
    for device in ys:
        first.add(total.at[0, :, 0:LANE], panel.at[col, 0], device)
    for device in ys:
        rest.add(total.at[1:, :, 0:LANE], panel.at[col, 1:], device)
    first.start()
    for q in range(1, cycles):
        assemble(0, q)
    panel[pl.ds(col, 1), 0] = total[0:1, :, 0:LANE]
    dz, dx, dc = Sends(s_dz, r_dz), Sends(s_dx, r_dx), Sends(s_dc, r_dc)
    az, ax, ac = Sends(s_az, r_az), Sends(s_ax, r_ax), Sends(s_ac, r_ac)
    mine = pltpu.make_async_copy(total.at[0, :, LANE:], across.at[zh, x, zl, core], local.at[1])
    mine.start()
    first.arrived()
    placed = pltpu.make_async_copy(panel.at[:, 0], corner.at[:, zh, x, zl, core], local.at[2])
    placed.start()
    for device in zs:
        dz.add(panel.at[:, 0], corner.at[:, zh, x, zl, core], device)
    dz.start()
    sibling.copies[1].wait_recv()
    for p in range(1, cycles):
        assemble(p, 0)
    placed.wait()
    mine.wait()
    dz.arrived()
    for device in xs:
        for a in range(2):
            for b in range(4):
                piece = corner.at[:, a, x, b, core]
                dx.add(piece, piece, device)
    dx.start()
    rest.start()
    panel[pl.ds(col, 1), 1:] = total[1:, :, 0:LANE][None]
    for device in zs:
        az.add(total.at[0, :, LANE:], across.at[zh, x, zl, core], device)
    dx.arrived()
    for a in range(2):
        for b in range(4):
            for c in range(4):
                piece = corner.at[:, a, b, c, core]
                dc.add(piece, piece, other)
    dc.start()
    az.start()
    for device in xs:
        for a in range(2):
            for b in range(4):
                piece = across.at[a, x, b, core]
                ax.add(piece, piece, device)
    for a in range(2):
        for b in range(4):
            for c in range(4):
                piece = across.at[a, b, c, core]
                ac.add(piece, piece, other)
    dc.arrived()
    for i in range(4):
        matrix[:, i * LANE : (i + 1) * LANE] = corner[i].reshape(WIDTH, LANE)

    def hook(k):
        @pl.when(k == 0)
        def _():
            az.arrived()
            ax.start()

        @pl.when(k == 2)
        def _():
            ax.arrived()
            ac.start()

    inverse_factor(matrix, block, strip, hook)
    sibling.copies[2].wait_recv()
    for p in range(1, cycles):
        for q in range(1, cycles):
            assemble(p, q)
    rest.arrived()
    for i in range(4):
        wide[:, i * LANE : (i + 1) * LANE] = panel[i].reshape(cycles * SUB, LANE)
    whole[...] = mm_t(wide[...], matrix[...])
    factor[...] = whole[:, pl.ds(pl.multiple_of(col * LANE, LANE), LANE)]
    wide[...] = mm(whole[...], matrix[...])
    ac.arrived()
    width = border * LANE
    for begin in range(0, width, 2 * LANE):
        size = min(2 * LANE, width - begin)
        product = mm(
            wide[SUB:, :], across[:, :, :, :, :, begin : begin + size].reshape(WIDTH, size)
        ).reshape(border, SUB, size)
        tail[:, :, begin : begin + size] = (
            total[1:, :, LANE + begin : LANE + begin + size] - product
        )
    for stage in (sibling, first, rest, dz, dx, dc, az, ax, ac):
        stage.left()


def pairs(counts):
    return [pltpu.SemaphoreType.DMA((n,)) for n in counts for _ in range(2)]


def shards(child_front, parent_front, border_map):
    cycles = child_front.shape[1]
    border = cycles - 1
    vmem = pl.BlockSpec(memory_space=pltpu.VMEM)
    smem = pl.BlockSpec(memory_space=pltpu.SMEM)
    front = child_front.reshape(cycles, CHILDREN, SUB, cycles * LANE)
    work = [
        pltpu.VMEM((WIDTH, WIDTH), F32),
        pltpu.VMEM((LANE, LANE), F32),
        pltpu.VMEM((LANE, WIDTH), F32),
    ]
    child_factor, update = pl.pallas_call(
        child_kernel,
        out_shape=(
            jax.ShapeDtypeStruct((cycles * CHILDREN * SUB, LANE), F32),
            jax.ShapeDtypeStruct((CHILDREN, border, SUB, border * LANE), F32),
        ),
        in_specs=[vmem],
        out_specs=(vmem, vmem),
        scratch_shapes=[
            pltpu.VMEM((4, cycles, CHILDREN, SUB, LANE), F32),
            pltpu.VMEM((4, 2, 4, CHILDREN, 2, 2, SUB, LANE), F32),
            pltpu.VMEM((2, 4, CHILDREN, 2, 2, SUB, border * LANE), F32),
            *work,
            pltpu.VMEM((cycles * CHILDREN * SUB, WIDTH), F32),
            pltpu.VMEM((cycles * CHILDREN * SUB, WIDTH), F32),
            pltpu.SemaphoreType.DMA((3,)),
            *pairs((3, 3, 3, 12, 16, 3, 12, 16)),
        ],
        compiler_params=pltpu.CompilerParams(collective_id=0, has_side_effects=True),
        name="child_panel",
    )(front)
    parent_cycles = parent_front.shape[0]
    tail_cycles = parent_cycles - 1
    parent_factor, tail = pl.pallas_call(
        parent_kernel,
        out_shape=(
            jax.ShapeDtypeStruct((parent_cycles * SUB, LANE), F32),
            jax.ShapeDtypeStruct((tail_cycles, SUB, tail_cycles * LANE), F32),
        ),
        in_specs=[smem, vmem, vmem],
        out_specs=(vmem, vmem),
        scratch_shapes=[
            pltpu.VMEM((border, SUB, border * LANE), F32),
            pltpu.VMEM((parent_cycles, SUB, parent_cycles * LANE), F32),
            pltpu.VMEM((4, parent_cycles, SUB, LANE), F32),
            pltpu.VMEM((4, 2, 4, 4, 2, SUB, LANE), F32),
            pltpu.VMEM((2, 4, 4, 2, SUB, tail_cycles * LANE), F32),
            *work,
            pltpu.VMEM((parent_cycles * SUB, WIDTH), F32),
            pltpu.VMEM((parent_cycles * SUB, WIDTH), F32),
            pltpu.SemaphoreType.DMA((3,)),
            *pairs((3, 3, 3, 7, 24, 32, 7, 24, 32)),
        ],
        compiler_params=pltpu.CompilerParams(collective_id=1, has_side_effects=True),
        name="parent_panel",
    )(border_map, update, parent_front.reshape(parent_cycles, SUB, parent_cycles * LANE))
    return (
        child_factor.reshape(1, cycles, 1, CHILDREN, SUB, 1, 1, LANE),
        parent_factor.reshape(parent_cycles, 1, 1, SUB, 1, 1, LANE),
        tail.reshape(tail_cycles, 1, 1, SUB, tail_cycles, 1, LANE),
    )


def solution(mesh):
    return jax.shard_map(
        shards,
        mesh=mesh,
        in_specs=(
            P("cube", None, "row", None, None, None, "col", None),
            P(None, "row", "cube", None, None, "col", None),
            P(),
        ),
        out_specs=(
            P("cube", None, "row", None, None, None, "col", None),
            P(None, "row", "cube", None, None, "col", None),
            P(None, "row", "cube", None, None, "col", None),
        ),
        check_vma=False,
    )
```

time: 1040 us -> 152 us (0.15)
  waiting for transfers between devices: 631 us -> 0 us
  other arithmetic: 250 us -> 5.58 us
  Pallas kernels: 0 us -> 139 us
  matrix products: 43.2 us -> 0 us
  blocking collectives: 42.8 us -> 0 us
  local copies, waits for them, and re-layouts: 38.4 us -> 5.68 us
  between operations: 19.9 us -> 0.68 us
    all_gather x4 -> x0, waiting for transfers between devices: 605 us -> none  [the longest x1 506 us: shards(): lax.all_gather(corner[None], ('cube', 'row', 'col'), axis=0, tiled=True)]
    another operation x36 -> x0, other arithmetic: 241 us -> none  [the longest x29 160 us: lower_inverse(): lower = jnp.linalg.cholesky(diagonal)]
    pallas_call x0 -> x2, Pallas kernels: none -> 139 us  [the longest x1 80.4 us: shards(): pl.pallas_call(parent_kernel, out_shape=(jax.ShapeDtypeStruct((parent_cyc...]
    all_gather x3 -> x0, blocking collectives: 42.8 us -> none  [the longest x1 19.6 us: shards(): partial_rows = lax.all_gather(top[None, None], 'cube', axis=1, tiled=True)]
    ppermute x3 -> x0, waiting for transfers between devices: 26 us -> none  [partner(): return lax.ppermute(block, axis, route)]
    another operation x37 -> x0, local copies, waits for them, and re-layouts: 24.4 us -> none  [the longest x28 22 us: lower_inverse(): return jax.scipy.linalg.solve_triangular(lower, identity, lower=True)]
    dot_general x8 -> x0, matrix products: 22.6 us -> none  [the longest x1 7.3 us: shards(): across = jnp.dot(mixing, rows_whole, precision=HIGHEST)]
    another operation x26 -> x0, matrix products: 20.6 us -> none  [the longest x12 10.9 us: lower_inverse(): lower = jnp.linalg.cholesky(diagonal)]
  transfers between devices with their start and end apart: 7 -> 0, of which waited for: 6 -> 0; matrix products, arithmetic and copies ran while one was open for 14% -> 0% of each run, Pallas kernels for 0% -> 0%
where the time goes in v2:
time: 152 us; the launch traced here: 151 us
  Pallas kernels  139 us (91%)
  local copies, waits for them, and re-layouts  5.68 us (4%)
  other arithmetic  5.58 us (4%)
    pallas_call x1, Pallas kernels, shards(): pl.pallas_call(parent_kernel, out_shape=(jax.ShapeDtypeStruct((parent_cyc...  80.4 us
    pallas_call x1, Pallas kernels, shards(): pl.pallas_call(child_kernel, out_shape=(jax.ShapeDtypeStruct((cycles * CH...  58.7 us
    unnamed x2, other arithmetic  5.58 us
    unnamed x9, local copies, waits for them, and re-layouts  3.61 us

profile of v2, /device:TPU:1, one launch (start us, length us, event | category | flops | bytes accessed | tf_op | source)
XLA Modules:
  0.0 151.0 jit_solution(4594503586419991499)
XLA Ops:
  0.6 4.2 %reduce = f32[12,2,8,12,128]{4,3,2,1,0:T(8,128)S(1)} reduce(f32[1,12,1,2,8,12,1,128]{7,6,5,4,3,2,1,0:T(1,128)} %param.3, f32[]{:T(128)} %constant.2), dimensions={0,2,6}, to_apply=%param.3.reduce_sub_computation | reduce | bytes 2359300 | tf_op args[0]
  4.8 1.2 reshape.21.front
  6.0 0.0 copy-start
  6.0 58.7 %child_panel.1 = (f32[192,128]{1,0:T(8,128)}, f32[2,11,8,1408]{3,2,1,0:T(8,128)}) custom-call(f32[12,2,8,1536]{3,2,1,0:T(8,128)} %reshape.21.front), custom_call_target="tpu_custom_call" | custom-call | tf_op jit(solution)/shard_map/child_panel/pallas_call | solution.py:409
  64.7 0.0 copy-done
  64.7 1.4 reduce.1
  66.1 0.9 reshape.23.front
  67.0 0.0 copy-start.1
  67.0 80.4 %parent_panel.1 = (f32[96,128]{1,0:T(8,128)}, f32[11,8,1408]{2,1,0:T(8,128)}) custom-call(s32[2,11]{1,0:T(2,128)} %border_map.1, f32[2,11,8,1408]{3,2,1,0:T(8,128)} %get-tuple-element.8.update, f32[12,8,1536]{2,1,0:T(8,128)} %reshape.23.front), custom_call_target="tpu_custom_call" | custom-call | tf_op jit(solution)/shard_map/parent_panel/pallas_call | solution.py:432
  147.4 0.0 copy-start.2
  147.4 2.3 %copy.8 = f32[11,1,1,8,11,1,128]{6,5,4,3,2,1,0:T(1,128)} copy(f32[11,1,1,8,11,1,128]{6,3,4,0,5,2,1:T(8,128)} %bitcast.7) | data formatting | bytes 991232
  149.8 0.0 copy-done.1
  149.8 0.6 copy.11
  150.4 0.0 copy-done.2
  150.4 0.6 copy.12
Async XLA Ops:
  6.0 58.7 %copy-start = (f32[12,1,1,8,12,1,128]{6,5,4,3,2,1,0:T(1,128)S(1)}, f32[12,1,1,8,12,1,128]{6,5,4,3,2,1,0:T(1,128)}, u32[]{:S(2)}) copy-start(f32[12,1,1,8,12,1,128]{6,5,4,3,2,1,0:T(1,128)} %param.4) | copy-start | bytes 1769476
  67.0 82.8 %copy-start.1 = (f32[192,128]{1,0:T(8,128)S(1)}, f32[192,128]{1,0:T(8,128)}, u32[]{:S(2)}) copy-start(f32[192,128]{1,0:T(8,128)} %get-tuple-element.7) | copy-start | bytes 294916
  147.4 3.0 %copy-start.2 = (f32[96,128]{1,0:T(8,128)S(1)}, f32[96,128]{1,0:T(8,128)}, u32[]{:S(2)}) copy-start(f32[96,128]{1,0:T(8,128)} %get-tuple-element.9) | copy-start | bytes 147460

commit v3 on v0

v3 whole, which is shorter than its diff:
```python
import functools

import jax
import jax.numpy as jnp
from jax import lax
from jax.experimental import pallas as pl
from jax.experimental.pallas import tpu as pltpu
from jax.sharding import PartitionSpec as P

CHILDREN = 2
SUB = 8
LANE = 128
WIDTH = 512
STEP = 8
HIGHEST = lax.Precision.HIGHEST
MESH = pl.DeviceIdType.MESH
F32 = jnp.float32


def mm(a, b):
    return jnp.dot(a, b, precision=HIGHEST, preferred_element_type=F32)


def mm_t(a, b):
    return lax.dot_general(
        a, b, (((1,), (1,)), ((), ())), precision=HIGHEST, preferred_element_type=F32
    )


def diagonal_inverse(tiles, out_ref, midway):
    rows = list(tiles)
    lane = lax.broadcasted_iota(jnp.int32, (SUB, LANE), 1)
    n = LANE // SUB
    for t in range(n):
        j = t * SUB
        if t == n // 2:
            midway()
        column = [
            {i: jnp.broadcast_to(rows[i][:, j + a : j + a + 1], (SUB, LANE)) for i in range(t, n)}
            for a in range(STEP)
        ]
        inside = (lane >= j) & (lane < j + STEP)
        right = []
        for a in range(STEP):
            row = jnp.broadcast_to(rows[t][a : a + 1, :], (SUB, LANE))
            right.append(jnp.where(lane == j + a, 1.0, jnp.where(inside, 0.0, row)))
        pivot = {
            (a, b): jnp.broadcast_to(column[b][t][a : a + 1, :], (SUB, LANE))
            for a in range(STEP)
            for b in range(a, STEP)
        }
        scaled = []
        for a in range(STEP):
            inverse = 1.0 / pivot[a, a]
            scaled.append(right[a] * inverse)
            row = jnp.where(lane <= j + a, right[a] * lax.rsqrt(pivot[a, a]), 0.0)
            out_ref[j + a : j + a + 1, :] = row[:1, :]
            for b in range(a + 1, STEP):
                ratio = pivot[a, b] * inverse
                right[b] = right[b] - pivot[a, b] * scaled[a]
                for d in range(b, STEP):
                    pivot[b, d] = pivot[b, d] - ratio * pivot[a, d]
                for i in range(t + 1, n):
                    column[b][i] = column[b][i] - column[a][i] * ratio
        for i in range(t + 1, n):
            rest = jnp.where(inside, 0.0, rows[i])
            for a in range(STEP):
                rest = rest - column[a][i] * scaled[a]
            rows[i] = rest


def inverse_factor(matrix, block, strip, midway, after):
    blocks = WIDTH // LANE

    def body(k, carry):
        here = pl.ds(pl.multiple_of(k * LANE, LANE), LANE)
        tiles = [
            matrix[pl.ds(pl.multiple_of(k * LANE + SUB * i, SUB), SUB), here]
            for i in range(LANE // SUB)
        ]
        diagonal_inverse(tiles, block, lambda: midway(k))
        after(k)
        strip[...] = mm(block[...], matrix[here, :])
        strip[:, here] = block[...]
        for i in range(1, blocks):
            below = slice(i * LANE, (i + 1) * LANE)

            @pl.when(k < i)
            def _():
                left = mm_t(matrix[below, here], block[...])
                matrix[below, here] = jnp.zeros((LANE, LANE), F32)
                matrix[below, :] = matrix[below, :] - mm(left, strip[...])

        for i in range(blocks):
            columns = slice(i * LANE, (i + 1) * LANE)
            matrix[here, columns] = jnp.where(k >= i, strip[:, columns], 0.0)
        return carry

    lax.fori_loop(0, blocks, body, 0)


class Sends:
    def __init__(self, send, recv):
        self.send, self.recv, self.copies = send, recv, []

    def add(self, src, dst, device):
        index = len(self.copies)
        copy = pltpu.make_async_remote_copy(
            src_ref=src,
            dst_ref=dst,
            send_sem=self.send.at[index],
            recv_sem=self.recv.at[index],
            device_id=device,
            device_id_type=MESH,
        )
        self.copies.append(copy)

    def start(self):
        for copy in self.copies:
            copy.start()

    def arrived(self):
        for copy in self.copies:
            copy.wait_recv()

    def left(self):
        for copy in self.copies:
            copy.wait_send()


def greet(peers):
    barrier = pltpu.get_barrier_semaphore()
    for device in peers:
        pl.semaphore_signal(barrier, inc=1, device_id=device, device_id_type=MESH)
    pl.semaphore_wait(barrier, len(peers))


def fill(matrix, corner, first, last):
    for i in range(first, last):
        matrix[:, i * LANE : (i + 1) * LANE] = corner[i].reshape(WIDTH, LANE)


class Panel:
    def __init__(self, corner, across, near, line, xs, other, own, band, core, sems):
        self.corner, self.across, self.core = corner, across, core
        self.near, self.line, self.xs, self.other = near, line, xs, other
        self.own, self.band = own, band
        (self.dz, self.dx0, self.dx1, self.dc0, self.dc1,
         self.az, self.ax0, self.ax1, self.ac0, self.ac1) = (Sends(*pair) for pair in sems)
        width = across.shape[-1]
        self.cut = width // 2 // LANE * LANE

    def stages(self):
        return (self.dz, self.dx0, self.dx1, self.dc0, self.dc1,
                self.az, self.ax0, self.ax1, self.ac0, self.ac1)

    def corner_out(self, tile):
        for device in self.near:
            self.dz.add(tile, self.own(self.corner), device)
        self.dz.start()

    def across_out(self, strip):
        for device in self.line:
            self.az.add(strip, self.band(self.across), device)
        self.az.start()

    def corner_on(self, along_x, along_core):
        self.dz.arrived()
        for device in self.xs:
            piece = along_x(self.corner, slice(0, 1))
            self.dx0.add(piece, piece, device)
        for device in self.xs:
            piece = along_x(self.corner, slice(1, 4))
            self.dx1.add(piece, piece, device)
        self.dx0.start()
        self.dx1.start()
        self.dx0.arrived()
        piece = along_core(self.corner, slice(0, 1))
        self.dc0.add(piece, piece, self.other)
        self.dc0.start()
        piece = along_core(self.corner, slice(1, 4))
        self.dc1.add(piece, piece, self.other)
        self.along = (along_x, along_core)

    def prepare_across(self, along_x, along_core):
        parts = (slice(0, self.cut), slice(self.cut, None))
        for part, ax, ac in zip(parts, (self.ax0, self.ax1), (self.ac0, self.ac1)):
            for device in self.xs:
                piece = along_x(self.across, part)
                ax.add(piece, piece, device)
            piece = along_core(self.across, part)
            ac.add(piece, piece, self.other)

    def factor(self, matrix, block, strip, also):
        self.dc0.arrived()
        fill(matrix, self.corner, 0, 1)

        def midway(k):
            @pl.when(k == 0)
            def _():
                self.dx1.arrived()
                self.dc1.start()
                self.az.arrived()
                self.ax0.start()
                self.ax1.start()
                also()

        def after(k):
            @pl.when(k == 0)
            def _():
                self.dc1.arrived()
                fill(matrix, self.corner, 1, 4)

            @pl.when(k == 1)
            def _():
                self.ax0.arrived()
                self.ac0.start()

            @pl.when(k == 2)
            def _():
                self.ax1.arrived()
                self.ac1.start()

        inverse_factor(matrix, block, strip, midway, after)


def kernel(
    border_map, child_in, parent_in, child_factor, parent_factor, tail,
    front, c_panel, c_corner, c_across, update,
    taken, total, p_panel, p_corner, p_across,
    matrix, block, strip, wide, whole, local, *sems,
):
    cube, row, col = lax.axis_index("cube"), lax.axis_index("row"), lax.axis_index("col")
    core, zl, child = cube % 2, cube // 2, cube // 4
    half = zl % 2
    x, zh = row % 4, row // 4
    cycles = front.shape[0]
    border = cycles - 1
    width = border * LANE

    def at(dz, dh, dy):
        return ((zl + dz) % 4 * 2 + core, (zh + dh) % 2 * 4 + x, (col + dy) % 4)

    def at_half(dz, dh, dy):
        return (child * 4 + (half + dz) % 2 * 2 + core, (zh + dh) % 2 * 4 + x, (col + dy) % 4)

    c_near = [at_half(a, b, d) for a in range(2) for b in range(2) for d in range(4) if a + b + d]
    p_near = [at(a, b, d) for a in range(4) for b in range(2) for d in range(4) if a + b + d]
    c_line = [at_half(a, b, 0) for a in range(2) for b in range(2) if a + b]
    p_line = [at(a, b, 0) for a in range(4) for b in range(2) if a + b]
    ys = [at(0, 0, d) for d in (1, 2, 3)]
    xs = [(cube, zh * 4 + (x + d) % 4, col) for d in (1, 2, 3)]
    other = (cube + 1 - 2 * core, row, col)
    partner = ((cube + 4) % 8, row, col)
    pairs_of = [(sems[2 * i], sems[2 * i + 1]) for i in range(len(sems) // 2)]
    greet(p_near + xs + [other])

    def lay(t):
        for h in range(CHILDREN):
            for s in range(cycles):
                start = ((t * CHILDREN + h) * SUB) * cycles + s
                front[t, h, :, s * LANE : (s + 1) * LANE] = child_in[
                    pl.ds(start, SUB, stride=cycles), :
                ]

    child_side = Panel(
        c_corner, c_across, c_near, c_line, xs, other,
        lambda ref: ref.at[col, zh, x, :, half, core],
        lambda ref: ref.at[zh, x, :, half, core],
        core, pairs_of[0:10],
    )
    lay(0)
    child_side.corner_out(front.at[0, :, :, 0:LANE])
    child_side.across_out(front.at[0, :, :, LANE:])
    own = front[0]
    c_corner[pl.ds(col, 1), pl.ds(zh, 1), pl.ds(x, 1), :, pl.ds(half, 1), pl.ds(core, 1)] = own[
        :, :, 0:LANE
    ].reshape(1, 1, 1, CHILDREN, 1, 1, SUB, LANE)
    c_across[pl.ds(zh, 1), pl.ds(x, 1), :, pl.ds(half, 1), pl.ds(core, 1)] = own[
        :, :, LANE:
    ].reshape(1, 1, CHILDREN, 1, 1, SUB, width)
    for t in range(1, cycles):
        lay(t)
    c_rest = Sends(*pairs_of[20])
    for device in ys:
        c_rest.add(front.at[:, :, :, 0:LANE], c_panel.at[col], device)
    c_rest.start()
    c_panel[pl.ds(col, 1)] = front[:, :, :, 0:LANE][None]
    child_side.corner_on(
        lambda ref, part: ref.at[part, :, x, :, :, core],
        lambda ref, part: ref.at[part, :, :, :, :, core],
    )
    child_side.prepare_across(
        lambda ref, part: ref.at[:, x, :, :, core, :, part],
        lambda ref, part: ref.at[:, :, :, :, core, :, part],
    )
    child_side.factor(matrix, block, strip, lambda: None)

    c_rest.arrived()
    for i in range(4):
        wide[:, i * LANE : (i + 1) * LANE] = c_panel[i].reshape(cycles * CHILDREN * SUB, LANE)
    whole[...] = mm_t(wide[...], matrix[...])
    wide[...] = mm(whole[...], matrix[...])
    child_side.ac0.arrived()

    def child_update(first, last, begin, end):
        for left in range(begin, end, 2 * LANE):
            size = min(2 * LANE, end - left)
            product = mm(
                wide[(first + 1) * CHILDREN * SUB : (last + 1) * CHILDREN * SUB, :],
                c_across[:, :, :, :, :, :, left : left + size].reshape(WIDTH, size),
            ).reshape(last - first, CHILDREN, SUB, size)
            for h in range(CHILDREN):
                update[h, first:last, :, left : left + size] = (
                    front[first + 1 : last + 1, h, :, LANE + left : LANE + left + size]
                    - product[:, h]
                )

    sibling = Sends(*pairs_of[21])
    for rows, columns in (
        (slice(0, 1), slice(0, LANE)),
        (slice(0, 1), slice(LANE, None)),
        (slice(1, None), slice(0, LANE)),
        (slice(1, None), slice(LANE, None)),
    ):
        sibling.add(
            update.at[1 - child, rows, :, columns], taken.at[rows, :, columns], partner
        )
    child_update(0, 1, 0, LANE)
    sibling.copies[0].start()
    child_side.ac1.arrived()
    child_update(0, 1, LANE, width)
    sibling.copies[1].start()
    child_update(1, border, 0, LANE)
    sibling.copies[2].start()

    holes = []
    for index in (child, 1 - child):
        hole = cycles * (cycles - 1) // 2
        for i in range(border):
            hole = hole - border_map[index, i]
        holes.append(hole)

    def shifted(pick, hole, p):
        if p == 0:
            return jnp.where(hole > 0, pick(0), 0.0)
        if p == border:
            return jnp.where(hole < p, pick(p - 1), 0.0)
        return jnp.where(hole > p, pick(p), jnp.where(hole < p, pick(p - 1), 0.0))

    sources = (
        lambda i, j: update[child, i, :, j * LANE : (j + 1) * LANE],
        lambda i, j: taken[i, :, j * LANE : (j + 1) * LANE],
    )

    def assemble(p, q):
        value = parent_in[pl.ds(p * SUB * cycles + q, SUB, stride=cycles), :]
        for source, hole in zip(sources, holes):
            value = value + shifted(lambda i: shifted(lambda j: source(i, j), hole, q), hole, p)
        total[p, :, q * LANE : (q + 1) * LANE] = value

    parent_side = Panel(
        p_corner, p_across, p_near, p_line, xs, other,
        lambda ref: ref.at[col, zh, x, zl, core],
        lambda ref: ref.at[zh, x, zl, core],
        core, pairs_of[10:20],
    )
    sibling.copies[0].wait_recv()
    assemble(0, 0)
    parent_side.corner_out(total.at[0, :, 0:LANE])
    sibling.copies[1].wait_recv()
    for q in range(1, cycles):
        assemble(0, q)
    parent_side.across_out(total.at[0, :, LANE:])
    own = total[0]
    p_corner[pl.ds(col, 1), pl.ds(zh, 1), pl.ds(x, 1), pl.ds(zl, 1), pl.ds(core, 1)] = own[
        :, 0:LANE
    ].reshape(1, 1, 1, 1, 1, SUB, LANE)
    p_across[pl.ds(zh, 1), pl.ds(x, 1), pl.ds(zl, 1), pl.ds(core, 1)] = own[:, LANE:].reshape(
        1, 1, 1, 1, SUB, width
    )
    sibling.copies[2].wait_recv()
    for p in range(1, cycles):
        assemble(p, 0)
    p_rest = Sends(*pairs_of[22])
    for device in ys:
        p_rest.add(total.at[:, :, 0:LANE], p_panel.at[col], device)
    p_rest.start()
    p_panel[pl.ds(col, 1)] = total[:, :, 0:LANE][None]
    child_update(1, border, LANE, width)
    child_factor[...] = whole[:, pl.ds(pl.multiple_of(col * LANE, LANE), LANE)]
    parent_side.corner_on(
        lambda ref, part: ref.at[part, :, x, :, core],
        lambda ref, part: ref.at[part, :, :, :, core],
    )
    parent_side.prepare_across(
        lambda ref, part: ref.at[:, x, :, core, :, part],
        lambda ref, part: ref.at[:, :, :, core, :, part],
    )
    parent_side.factor(matrix, block, strip, lambda: sibling.copies[3].start())

    p_rest.arrived()
    rows = cycles * SUB
    for i in range(4):
        wide[:rows, i * LANE : (i + 1) * LANE] = p_panel[i].reshape(rows, LANE)
    whole[:rows, :] = mm_t(wide[:rows, :], matrix[...])
    wide[:rows, :] = mm(whole[:rows, :], matrix[...])
    parent_factor[...] = whole[:rows, pl.ds(pl.multiple_of(col * LANE, LANE), LANE)]
    sibling.copies[3].wait_recv()
    for p in range(1, cycles):
        for q in range(1, cycles):
            assemble(p, q)
    parent_side.ac0.arrived()
    parent_side.ac1.arrived()
    for left in range(0, width, 2 * LANE):
        size = min(2 * LANE, width - left)
        product = mm(
            wide[SUB:rows, :], p_across[:, :, :, :, :, left : left + size].reshape(WIDTH, size)
        ).reshape(border, SUB, size)
        value = total[1:, :, LANE + left : LANE + left + size] - product
        for p in range(border):
            for q in range(size // LANE):
                tail[pl.ds(p * SUB * border + left // LANE + q, SUB, stride=border), :] = value[
                    p, :, q * LANE : (q + 1) * LANE
                ]
    for stage in (*child_side.stages(), *parent_side.stages(), c_rest, sibling, p_rest):
        stage.left()


def shards(child_front, parent_front, border_map):
    cycles = child_front.shape[1]
    border = cycles - 1
    vmem = pl.BlockSpec(memory_space=pltpu.VMEM)
    smem = pl.BlockSpec(memory_space=pltpu.SMEM)
    counts = [15, 3, 3, 1, 1, 3, 3, 3, 1, 1, 31, 3, 3, 1, 1, 7, 3, 3, 1, 1, 3, 4, 3]
    child_factor, parent_factor, tail = pl.pallas_call(
        kernel,
        out_shape=(
            jax.ShapeDtypeStruct((cycles * CHILDREN * SUB, LANE), F32),
            jax.ShapeDtypeStruct((cycles * SUB, LANE), F32),
            jax.ShapeDtypeStruct((border * SUB * border, LANE), F32),
        ),
        in_specs=[smem, vmem, vmem],
        out_specs=(vmem, vmem, vmem),
        scratch_shapes=[
            pltpu.VMEM((cycles, CHILDREN, SUB, cycles * LANE), F32),
            pltpu.VMEM((4, cycles, CHILDREN, SUB, LANE), F32),
            pltpu.VMEM((4, 2, 4, CHILDREN, 2, 2, SUB, LANE), F32),
            pltpu.VMEM((2, 4, CHILDREN, 2, 2, SUB, border * LANE), F32),
            pltpu.VMEM((CHILDREN, border, SUB, border * LANE), F32),
            pltpu.VMEM((border, SUB, border * LANE), F32),
            pltpu.VMEM((cycles, SUB, cycles * LANE), F32),
            pltpu.VMEM((4, cycles, SUB, LANE), F32),
            pltpu.VMEM((4, 2, 4, 4, 2, SUB, LANE), F32),
            pltpu.VMEM((2, 4, 4, 2, SUB, border * LANE), F32),
            pltpu.VMEM((WIDTH, WIDTH), F32),
            pltpu.VMEM((LANE, LANE), F32),
            pltpu.VMEM((LANE, WIDTH), F32),
            pltpu.VMEM((cycles * CHILDREN * SUB, WIDTH), F32),
            pltpu.VMEM((cycles * CHILDREN * SUB, WIDTH), F32),
            pltpu.SemaphoreType.DMA((1,)),
            *(pltpu.SemaphoreType.DMA((n,)) for n in counts for _ in range(2)),
        ],
        compiler_params=pltpu.CompilerParams(collective_id=0, has_side_effects=True),
        name="fronts",
    )(
        border_map,
        child_front.reshape(cycles * CHILDREN * SUB * cycles, LANE),
        parent_front.reshape(cycles * SUB * cycles, LANE),
    )
    return (
        child_factor.reshape(1, cycles, 1, CHILDREN, SUB, 1, 1, LANE),
        parent_factor.reshape(cycles, 1, 1, SUB, 1, 1, LANE),
        tail.reshape(border, 1, 1, SUB, border, 1, LANE),
    )


def solution(mesh):
    return jax.shard_map(
        shards,
        mesh=mesh,
        in_specs=(
            P("cube", None, "row", None, None, None, "col", None),
            P(None, "row", "cube", None, None, "col", None),
            P(),
        ),
        out_specs=(
            P("cube", None, "row", None, None, None, "col", None),
            P(None, "row", "cube", None, None, "col", None),
            P(None, "row", "cube", None, None, "col", None),
        ),
        check_vma=False,
    )
```

time: 1040 us -> 116 us (0.11)
  waiting for transfers between devices: 631 us -> 0 us
  other arithmetic: 250 us -> 0 us
  Pallas kernels: 0 us -> 110 us
  matrix products: 43.2 us -> 0 us
  blocking collectives: 42.8 us -> 0 us
  local copies, waits for them, and re-layouts: 38.4 us -> 4.86 us
  between operations: 19.9 us -> 0.64 us
    all_gather x4 -> x0, waiting for transfers between devices: 605 us -> none  [the longest x1 506 us: shards(): lax.all_gather(corner[None], ('cube', 'row', 'col'), axis=0, tiled=True)]
    another operation x36 -> x0, other arithmetic: 241 us -> none  [the longest x29 160 us: lower_inverse(): lower = jnp.linalg.cholesky(diagonal)]
    pallas_call x0 -> x1, Pallas kernels: none -> 110 us  [shards(): pl.pallas_call(kernel, out_shape=(jax.ShapeDtypeStruct((cycles * CHILDREN...]
    all_gather x3 -> x0, blocking collectives: 42.8 us -> none  [the longest x1 19.6 us: shards(): partial_rows = lax.all_gather(top[None, None], 'cube', axis=1, tiled=True)]
    ppermute x3 -> x0, waiting for transfers between devices: 26 us -> none  [partner(): return lax.ppermute(block, axis, route)]
    another operation x37 -> x0, local copies, waits for them, and re-layouts: 24.4 us -> none  [the longest x28 22 us: lower_inverse(): return jax.scipy.linalg.solve_triangular(lower, identity, lower=True)]
    dot_general x8 -> x0, matrix products: 22.6 us -> none  [the longest x1 7.3 us: shards(): across = jnp.dot(mixing, rows_whole, precision=HIGHEST)]
    another operation x26 -> x0, matrix products: 20.6 us -> none  [the longest x12 10.9 us: lower_inverse(): lower = jnp.linalg.cholesky(diagonal)]
  transfers between devices with their start and end apart: 7 -> 0, of which waited for: 6 -> 0; matrix products, arithmetic and copies ran while one was open for 14% -> 0% of each run, Pallas kernels for 0% -> 0%
where the time goes in v3:
time: 116 us
  Pallas kernels  110 us (95%)
  local copies, waits for them, and re-layouts  4.86 us (4%)
    pallas_call x1, Pallas kernels, shards(): pl.pallas_call(kernel, out_shape=(jax.ShapeDtypeStruct((cycles * CHILDREN...  110 us
    unnamed x3, local copies, waits for them, and re-layouts  4.86 us

profile of v3, /device:TPU:1, one launch (start us, length us, event | category | flops | bytes accessed | tf_op | source)
XLA Modules:
  0.0 115.9 jit_solution(9824852285045262138)
XLA Ops:
  0.6 110.5 %fronts.1 = (f32[192,128]{1,0:T(8,128)}, f32[96,128]{1,0:T(8,128)}, f32[968,128]{1,0:T(8,128)}) custom-call(s32[2,11]{1,0:T(2,128)} %border_map.1, f32[2304,128]{1,0:T(8,128)} %bitcast.9, f32[1152,128]{1,0:T(8,128)} %bitcast.10), custom_call_target="tpu_custom_call" | custom-call | tf_op jit(solution)/shard_map/fronts/pallas_call | solution.py:436
  111.1 1.5 %copy.15 = f32[1,12,1,2,8,1,1,128]{7,6,5,4,3,2,1,0:T(1,128)} copy(f32[1,12,1,2,8,1,1,128]{7,6,5,4,3,2,1,0:T(1,128)} %bitcast.12) | data formatting | bytes 196608
  112.6 1.4 %copy.16 = f32[12,1,1,8,1,1,128]{6,5,4,3,2,1,0:T(1,128)} copy(f32[12,1,1,8,1,1,128]{6,5,4,3,2,1,0:T(1,128)} %bitcast.13) | data formatting | bytes 98304
  114.1 1.9 %copy.17 = f32[11,1,1,8,11,1,128]{6,5,4,3,2,1,0:T(1,128)} copy(f32[11,1,1,8,11,1,128]{6,5,4,3,2,1,0:T(1,128)} %bitcast.11) | data formatting | bytes 991232

commit v4 on v3

--- a/solution.py
+++ b/solution.py
@@ -31,42 +31,54 @@
     rows = list(tiles)
     lane = lax.broadcasted_iota(jnp.int32, (SUB, LANE), 1)
     n = LANE // SUB
+
+    def across_lanes(tile, index):
+        picks = jnp.full((SUB, LANE), index, jnp.int32)
+        return jnp.take_along_axis(tile, picks, axis=1, mode="promise_in_bounds")
+
+    def across_rows(tile, index):
+        return jnp.broadcast_to(tile[index : index + 1, :], (SUB, LANE))
+
     for t in range(n):
         j = t * SUB
         if t == n // 2:
             midway()
-        column = [
-            {i: jnp.broadcast_to(rows[i][:, j + a : j + a + 1], (SUB, LANE)) for i in range(t, n)}
+        inside = (lane >= j) & (lane < j + STEP)
+        near = range(t + 1, min(n, t + 2))
+        column = [across_lanes(rows[t], j + a) for a in range(STEP)]
+        below = {i: [across_lanes(rows[i], j + a) for a in range(STEP)] for i in near}
+        rest = {i: jnp.where(inside, 0.0, rows[i]) for i in range(t + 1, n)}
+        right = [
+            jnp.where(lane == j + a, 1.0, jnp.where(inside, 0.0, across_rows(rows[t], a)))
             for a in range(STEP)
         ]
-        inside = (lane >= j) & (lane < j + STEP)
-        right = []
-        for a in range(STEP):
-            row = jnp.broadcast_to(rows[t][a : a + 1, :], (SUB, LANE))
-            right.append(jnp.where(lane == j + a, 1.0, jnp.where(inside, 0.0, row)))
         pivot = {
-            (a, b): jnp.broadcast_to(column[b][t][a : a + 1, :], (SUB, LANE))
-            for a in range(STEP)
-            for b in range(a, STEP)
+            (a, b): across_rows(column[b], a) for a in range(STEP) for b in range(a, STEP)
         }
-        scaled = []
+        scaled, ratio = [], {}
         for a in range(STEP):
             inverse = 1.0 / pivot[a, a]
             scaled.append(right[a] * inverse)
             row = jnp.where(lane <= j + a, right[a] * lax.rsqrt(pivot[a, a]), 0.0)
             out_ref[j + a : j + a + 1, :] = row[:1, :]
             for b in range(a + 1, STEP):
-                ratio = pivot[a, b] * inverse
+                ratio[a, b] = pivot[a, b] * inverse
+                for d in range(b, STEP):
+                    pivot[b, d] = pivot[b, d] - ratio[a, b] * pivot[a, d]
                 right[b] = right[b] - pivot[a, b] * scaled[a]
-                for d in range(b, STEP):
-                    pivot[b, d] = pivot[b, d] - ratio * pivot[a, d]
-                for i in range(t + 1, n):
-                    column[b][i] = column[b][i] - column[a][i] * ratio
+                for i in near:
+                    below[i][b] = below[i][b] - below[i][a] * ratio[a, b]
+            for i in near:
+                rest[i] = rest[i] - below[i][a] * scaled[a]
+        if t + 2 < n:
+            for b in range(STEP - 1, 0, -1):
+                for a in range(b):
+                    scaled[a] = scaled[a] - ratio[a, b] * scaled[b]
+        for i in range(t + 2, n):
+            for a in range(STEP):
+                rest[i] = rest[i] - across_lanes(rows[i], j + a) * scaled[a]
         for i in range(t + 1, n):
-            rest = jnp.where(inside, 0.0, rows[i])
-            for a in range(STEP):
-                rest = rest - column[a][i] * scaled[a]
-            rows[i] = rest
+            rows[i] = rest[i]
 
 
 def inverse_factor(matrix, block, strip, midway, after):
@@ -141,18 +153,18 @@
 
 
 class Panel:
-    def __init__(self, corner, across, near, line, xs, other, own, band, core, sems):
-        self.corner, self.across, self.core = corner, across, core
+    def __init__(self, corner, across, near, line, xs, other, own, band, sems):
+        self.corner, self.across = corner, across
         self.near, self.line, self.xs, self.other = near, line, xs, other
         self.own, self.band = own, band
-        (self.dz, self.dx0, self.dx1, self.dc0, self.dc1,
-         self.az, self.ax0, self.ax1, self.ac0, self.ac1) = (Sends(*pair) for pair in sems)
-        width = across.shape[-1]
-        self.cut = width // 2 // LANE * LANE
+        (self.dz, self.dx0, self.dx1, self.dc0, self.dc1, self.az, self.ring, self.on, self.ac) = (
+            Sends(*pair) for pair in sems
+        )
 
     def stages(self):
-        return (self.dz, self.dx0, self.dx1, self.dc0, self.dc1,
-                self.az, self.ax0, self.ax1, self.ac0, self.ac1)
+        return (
+            self.dz, self.dx0, self.dx1, self.dc0, self.dc1, self.az, self.ring, self.on, self.ac
+        )
 
     def corner_out(self, tile):
         for device in self.near:
@@ -166,30 +178,31 @@
 
     def corner_on(self, along_x, along_core):
         self.dz.arrived()
-        for device in self.xs:
-            piece = along_x(self.corner, slice(0, 1))
-            self.dx0.add(piece, piece, device)
-        for device in self.xs:
-            piece = along_x(self.corner, slice(1, 4))
-            self.dx1.add(piece, piece, device)
-        self.dx0.start()
-        self.dx1.start()
+        for stage, part in ((self.dx0, slice(0, 1)), (self.dx1, slice(1, 4))):
+            piece = along_x(self.corner, part)
+            for device in self.xs:
+                stage.add(piece, piece, device)
+            stage.start()
+        for stage, part in ((self.dc0, slice(0, 1)), (self.dc1, slice(1, 4))):
+            piece = along_core(self.corner, part)
+            stage.add(piece, piece, self.other)
         self.dx0.arrived()
-        piece = along_core(self.corner, slice(0, 1))
-        self.dc0.add(piece, piece, self.other)
         self.dc0.start()
-        piece = along_core(self.corner, slice(1, 4))
-        self.dc1.add(piece, piece, self.other)
-        self.along = (along_x, along_core)
-
-    def prepare_across(self, along_x, along_core):
-        parts = (slice(0, self.cut), slice(self.cut, None))
-        for part, ax, ac in zip(parts, (self.ax0, self.ax1), (self.ac0, self.ac1)):
-            for device in self.xs:
-                piece = along_x(self.across, part)
-                ax.add(piece, piece, device)
-            piece = along_core(self.across, part)
-            ac.add(piece, piece, self.other)
+
+    def prepare_across(self, x, block):
+        cut = self.across.shape[-1] // 2 // LANE * LANE
+        half = (slice(0, cut), slice(cut, None))
+        right, left = self.xs[0], self.xs[2]
+        for device, part in ((right, 0), (left, 1), (right, 1), (left, 0)):
+            piece = block(x, half[part])
+            self.ring.add(piece, piece, device)
+        piece = block((x + 3) % 4, half[0])
+        self.on.add(piece, piece, right)
+        piece = block((x + 1) % 4, half[1])
+        self.on.add(piece, piece, left)
+        for d in (0, 1, 3, 2):
+            piece = block((x + d) % 4, slice(None))
+            self.ac.add(piece, piece, self.other)
 
     def factor(self, matrix, block, strip, also):
         self.dc0.arrived()
@@ -201,9 +214,13 @@
                 self.dx1.arrived()
                 self.dc1.start()
                 self.az.arrived()
-                self.ax0.start()
-                self.ax1.start()
+                self.ring.start()
                 also()
+
+            @pl.when(k == 3)
+            def _():
+                self.on.arrived()
+                self.ac.copies[3].start()
 
         def after(k):
             @pl.when(k == 0)
@@ -213,20 +230,23 @@
 
             @pl.when(k == 1)
             def _():
-                self.ax0.arrived()
-                self.ac0.start()
+                for copy in self.ring.copies[:2]:
+                    copy.wait_recv()
+                self.on.start()
 
             @pl.when(k == 2)
             def _():
-                self.ax1.arrived()
-                self.ac1.start()
+                for copy in self.ring.copies[2:]:
+                    copy.wait_recv()
+                for copy in self.ac.copies[:3]:
+                    copy.start()
 
         inverse_factor(matrix, block, strip, midway, after)
 
 
 def kernel(
-    border_map, child_in, parent_in, child_factor, parent_factor, tail,
-    front, c_panel, c_corner, c_across, update,
+    border_map, child_hbm, parent_hbm, child_factor, parent_factor, tail,
+    child_in, parent_in, front, c_panel, c_corner, c_across, update,
     taken, total, p_panel, p_corner, p_across,
     matrix, block, strip, wide, whole, local, *sems,
 ):
@@ -253,8 +273,6 @@
     other = (cube + 1 - 2 * core, row, col)
     partner = ((cube + 4) % 8, row, col)
     pairs_of = [(sems[2 * i], sems[2 * i + 1]) for i in range(len(sems) // 2)]
-    greet(p_near + xs + [other])
-
     def lay(t):
         for h in range(CHILDREN):
             for s in range(cycles):
@@ -263,13 +281,24 @@
                     pl.ds(start, SUB, stride=cycles), :
                 ]
 
+    head = CHILDREN * SUB * cycles
+    loads = [
+        pltpu.make_async_copy(child_hbm.at[:head], child_in.at[:head], local.at[0]),
+        pltpu.make_async_copy(child_hbm.at[head:], child_in.at[head:], local.at[1]),
+        pltpu.make_async_copy(parent_hbm, parent_in, local.at[2]),
+    ]
+    for load in loads:
+        load.start()
+    loads[0].wait()
+    lay(0)
+    greet(p_near + xs + [other])
+
     child_side = Panel(
         c_corner, c_across, c_near, c_line, xs, other,
         lambda ref: ref.at[col, zh, x, :, half, core],
         lambda ref: ref.at[zh, x, :, half, core],
-        core, pairs_of[0:10],
-    )
-    lay(0)
+        pairs_of[0:9],
+    )
     child_side.corner_out(front.at[0, :, :, 0:LANE])
     child_side.across_out(front.at[0, :, :, LANE:])
     own = front[0]
@@ -279,9 +308,11 @@
     c_across[pl.ds(zh, 1), pl.ds(x, 1), :, pl.ds(half, 1), pl.ds(core, 1)] = own[
         :, :, LANE:
     ].reshape(1, 1, CHILDREN, 1, 1, SUB, width)
+    loads[1].wait()
     for t in range(1, cycles):
         lay(t)
-    c_rest = Sends(*pairs_of[20])
+    loads[2].wait()
+    c_rest = Sends(*pairs_of[18])
     for device in ys:
         c_rest.add(front.at[:, :, :, 0:LANE], c_panel.at[col], device)
     c_rest.start()
@@ -290,10 +321,7 @@
         lambda ref, part: ref.at[part, :, x, :, :, core],
         lambda ref, part: ref.at[part, :, :, :, :, core],
     )
-    child_side.prepare_across(
-        lambda ref, part: ref.at[:, x, :, :, core, :, part],
-        lambda ref, part: ref.at[:, :, :, :, core, :, part],
-    )
+    child_side.prepare_across(x, lambda at_x, part: c_across.at[:, at_x, :, :, core, :, part])
     child_side.factor(matrix, block, strip, lambda: None)
 
     c_rest.arrived()
@@ -301,7 +329,7 @@
         wide[:, i * LANE : (i + 1) * LANE] = c_panel[i].reshape(cycles * CHILDREN * SUB, LANE)
     whole[...] = mm_t(wide[...], matrix[...])
     wide[...] = mm(whole[...], matrix[...])
-    child_side.ac0.arrived()
+    child_side.ac.arrived()
 
     def child_update(first, last, begin, end):
         for left in range(begin, end, 2 * LANE):
@@ -316,7 +344,7 @@
                     - product[:, h]
                 )
 
-    sibling = Sends(*pairs_of[21])
+    sibling = Sends(*pairs_of[19])
     for rows, columns in (
         (slice(0, 1), slice(0, LANE)),
         (slice(0, 1), slice(LANE, None)),
@@ -328,7 +356,6 @@
         )
     child_update(0, 1, 0, LANE)
     sibling.copies[0].start()
-    child_side.ac1.arrived()
     child_update(0, 1, LANE, width)
     sibling.copies[1].start()
     child_update(1, border, 0, LANE)
@@ -363,7 +390,7 @@
         p_corner, p_across, p_near, p_line, xs, other,
         lambda ref: ref.at[col, zh, x, zl, core],
         lambda ref: ref.at[zh, x, zl, core],
-        core, pairs_of[10:20],
+        pairs_of[9:18],
     )
     sibling.copies[0].wait_recv()
     assemble(0, 0)
@@ -382,7 +409,7 @@
     sibling.copies[2].wait_recv()
     for p in range(1, cycles):
         assemble(p, 0)
-    p_rest = Sends(*pairs_of[22])
+    p_rest = Sends(*pairs_of[20])
     for device in ys:
         p_rest.add(total.at[:, :, 0:LANE], p_panel.at[col], device)
     p_rest.start()
@@ -393,10 +420,7 @@
         lambda ref, part: ref.at[part, :, x, :, core],
         lambda ref, part: ref.at[part, :, :, :, core],
     )
-    parent_side.prepare_across(
-        lambda ref, part: ref.at[:, x, :, core, :, part],
-        lambda ref, part: ref.at[:, :, :, core, :, part],
-    )
+    parent_side.prepare_across(x, lambda at_x, part: p_across.at[:, at_x, :, core, :, part])
     parent_side.factor(matrix, block, strip, lambda: sibling.copies[3].start())
 
     p_rest.arrived()
@@ -410,8 +434,7 @@
     for p in range(1, cycles):
         for q in range(1, cycles):
             assemble(p, q)
-    parent_side.ac0.arrived()
-    parent_side.ac1.arrived()
+    parent_side.ac.arrived()
     for left in range(0, width, 2 * LANE):
         size = min(2 * LANE, width - left)
         product = mm(
@@ -427,12 +450,19 @@
         stage.left()
 
 
+def hand_on(first, second, third, first_out, second_out, third_out):
+    first_out[...] = first[...]
+    second_out[...] = second[...]
+    third_out[...] = third[...]
+
+
 def shards(child_front, parent_front, border_map):
     cycles = child_front.shape[1]
     border = cycles - 1
     vmem = pl.BlockSpec(memory_space=pltpu.VMEM)
     smem = pl.BlockSpec(memory_space=pltpu.SMEM)
-    counts = [15, 3, 3, 1, 1, 3, 3, 3, 1, 1, 31, 3, 3, 1, 1, 7, 3, 3, 1, 1, 3, 4, 3]
+    kept = pl.BlockSpec(memory_space=pl.ANY)
+    counts = [15, 3, 3, 1, 1, 3, 4, 2, 4, 31, 3, 3, 1, 1, 7, 4, 2, 4, 3, 4, 3]
     child_factor, parent_factor, tail = pl.pallas_call(
         kernel,
         out_shape=(
@@ -440,9 +470,11 @@
             jax.ShapeDtypeStruct((cycles * SUB, LANE), F32),
             jax.ShapeDtypeStruct((border * SUB * border, LANE), F32),
         ),
-        in_specs=[smem, vmem, vmem],
+        in_specs=[smem, kept, kept],
         out_specs=(vmem, vmem, vmem),
         scratch_shapes=[
+            pltpu.VMEM((cycles * CHILDREN * SUB * cycles, LANE), F32),
+            pltpu.VMEM((cycles * SUB * cycles, LANE), F32),
             pltpu.VMEM((cycles, CHILDREN, SUB, cycles * LANE), F32),
             pltpu.VMEM((4, cycles, CHILDREN, SUB, LANE), F32),
             pltpu.VMEM((4, 2, 4, CHILDREN, 2, 2, SUB, LANE), F32),
@@ -458,7 +490,7 @@
             pltpu.VMEM((LANE, WIDTH), F32),
             pltpu.VMEM((cycles * CHILDREN * SUB, WIDTH), F32),
             pltpu.VMEM((cycles * CHILDREN * SUB, WIDTH), F32),
-            pltpu.SemaphoreType.DMA((1,)),
+            pltpu.SemaphoreType.DMA((3,)),
             *(pltpu.SemaphoreType.DMA((n,)) for n in counts for _ in range(2)),
         ],
         compiler_params=pltpu.CompilerParams(collective_id=0, has_side_effects=True),
@@ -468,6 +500,15 @@
         child_front.reshape(cycles * CHILDREN * SUB * cycles, LANE),
         parent_front.reshape(cycles * SUB * cycles, LANE),
     )
+    child_factor, parent_factor, tail = pl.pallas_call(
+        hand_on,
+        out_shape=tuple(
+            jax.ShapeDtypeStruct(value.shape, F32) for value in (child_factor, parent_factor, tail)
+        ),
+        in_specs=[vmem] * 3,
+        out_specs=(vmem,) * 3,
+        name="hand_on",
+    )(child_factor, parent_factor, tail)
     return (
         child_factor.reshape(1, cycles, 1, CHILDREN, SUB, 1, 1, LANE),
         parent_factor.reshape(cycles, 1, 1, SUB, 1, 1, LANE),

time: 116 us -> 95.8 us (0.83)
  Pallas kernels: 110 us -> 95.1 us
  local copies, waits for them, and re-layouts: 4.86 us -> 0 us
    pallas_call x1, Pallas kernels: 110 us -> 93.1 us  [shards(): pl.pallas_call(kernel, out_shape=(jax.ShapeDtypeStruct((cycles * CHILDREN...]
    unnamed x3 -> x0, local copies, waits for them, and re-layouts: 4.86 us -> none
    pallas_call x0 -> x1, Pallas kernels: none -> 1.94 us  [shards(): pl.pallas_call(hand_on, out_shape=tuple((jax.ShapeDtypeStruct(value.shape...]
where the time goes in v4:
time: 95.8 us; the launch traced here: 95.7 us
  Pallas kernels  95.1 us (99%)
    pallas_call x1, Pallas kernels, shards(): pl.pallas_call(kernel, out_shape=(jax.ShapeDtypeStruct((cycles * CHILDREN...  93.1 us
    pallas_call x1, Pallas kernels, shards(): pl.pallas_call(hand_on, out_shape=tuple((jax.ShapeDtypeStruct(value.shape...  1.94 us

profile of v4, /device:TPU:1, one launch (start us, length us, event | category | flops | bytes accessed | tf_op | source)
XLA Modules:
  0.0 95.7 jit_solution(4873767897262607799)
XLA Ops:
  0.6 93.1 %fronts.1 = (f32[192,128]{1,0:T(8,128)}, f32[96,128]{1,0:T(8,128)}, f32[968,128]{1,0:T(8,128)}) custom-call(s32[2,11]{1,0:T(2,128)} %border_map.1, f32[2304,128]{1,0:T(8,128)} %bitcast.9, f32[1152,128]{1,0:T(8,128)} %bitcast.10), custom_call_target="tpu_custom_call" | custom-call | tf_op jit(solution)/shard_map/fronts/pallas_call | solution.py:466
  93.8 1.9 %hand_on.1 = (f32[192,128]{1,0:T(8,128)}, f32[96,128]{1,0:T(8,128)}, f32[968,128]{1,0:T(8,128)}) custom-call(f32[192,128]{1,0:T(8,128)} %get-tuple-element.9.first, f32[96,128]{1,0:T(8,128)} %get-tuple-element.10.second, f32[968,128]{1,0:T(8,128)} %get-tuple-element.11.third), custom_call_target="tpu_custom_call" | custom-call | tf_op jit(solution)/shard_map/hand_on/pallas_call | solution.py:503

commit v5 on v4

--- a/solution.py
+++ b/solution.py
@@ -81,28 +81,26 @@
             rows[i] = rest[i]
 
 
-def inverse_factor(matrix, block, strip, midway, after):
+def inverse_factor(matrix, block, strip, low, midway, after):
     blocks = WIDTH // LANE
+    low[...] = jnp.zeros(low.shape, F32)
+    strip[...] = jnp.zeros(strip.shape, F32)
 
     def body(k, carry):
         here = pl.ds(pl.multiple_of(k * LANE, LANE), LANE)
-        tiles = [
-            matrix[pl.ds(pl.multiple_of(k * LANE + SUB * i, SUB), SUB), here]
-            for i in range(LANE // SUB)
-        ]
+        share = matrix[here, here] - mm(low[here, :], strip[:, here])
+        tiles = [share[SUB * i : SUB * (i + 1), :] for i in range(LANE // SUB)]
+        for i in range(1, blocks):
+            below = slice(i * LANE, (i + 1) * LANE)
+            matrix[below, :] = matrix[below, :] - mm(low[below, :], strip[...])
         diagonal_inverse(tiles, block, lambda: midway(k))
         after(k)
         strip[...] = mm(block[...], matrix[here, :])
         strip[:, here] = block[...]
         for i in range(1, blocks):
             below = slice(i * LANE, (i + 1) * LANE)
-
-            @pl.when(k < i)
-            def _():
-                left = mm_t(matrix[below, here], block[...])
-                matrix[below, here] = jnp.zeros((LANE, LANE), F32)
-                matrix[below, :] = matrix[below, :] - mm(left, strip[...])
-
+            low[below, :] = jnp.where(k < i, mm_t(matrix[below, here], block[...]), 0.0)
+            matrix[below, here] = jnp.where(k < i, 0.0, matrix[below, here])
         for i in range(blocks):
             columns = slice(i * LANE, (i + 1) * LANE)
             matrix[here, columns] = jnp.where(k >= i, strip[:, columns], 0.0)
@@ -153,7 +151,8 @@
 
 
 class Panel:
-    def __init__(self, corner, across, near, line, xs, other, own, band, sems):
+    def __init__(self, corner, across, near, line, xs, other, own, band, late, sems):
+        self.late = late
         self.corner, self.across = corner, across
         self.near, self.line, self.xs, self.other = near, line, xs, other
         self.own, self.band = own, band
@@ -174,7 +173,8 @@
     def across_out(self, strip):
         for device in self.line:
             self.az.add(strip, self.band(self.across), device)
-        self.az.start()
+        if not self.late:
+            self.az.start()
 
     def corner_on(self, along_x, along_core):
         self.dz.arrived()
@@ -186,6 +186,8 @@
         for stage, part in ((self.dc0, slice(0, 1)), (self.dc1, slice(1, 4))):
             piece = along_core(self.corner, part)
             stage.add(piece, piece, self.other)
+        if self.late:
+            self.az.start()
         self.dx0.arrived()
         self.dc0.start()
 
@@ -204,7 +206,7 @@
             piece = block((x + d) % 4, slice(None))
             self.ac.add(piece, piece, self.other)
 
-    def factor(self, matrix, block, strip, also):
+    def factor(self, matrix, block, strip, low, also):
         self.dc0.arrived()
         fill(matrix, self.corner, 0, 1)
 
@@ -213,8 +215,9 @@
             def _():
                 self.dx1.arrived()
                 self.dc1.start()
-                self.az.arrived()
-                self.ring.start()
+                if not self.late:
+                    self.az.arrived()
+                    self.ring.start()
                 also()
 
             @pl.when(k == 3)
@@ -225,6 +228,9 @@
         def after(k):
             @pl.when(k == 0)
             def _():
+                if self.late:
+                    self.az.arrived()
+                    self.ring.start()
                 self.dc1.arrived()
                 fill(matrix, self.corner, 1, 4)
 
@@ -241,14 +247,14 @@
                 for copy in self.ac.copies[:3]:
                     copy.start()
 
-        inverse_factor(matrix, block, strip, midway, after)
+        inverse_factor(matrix, block, strip, low, midway, after)
 
 
 def kernel(
     border_map, child_hbm, parent_hbm, child_factor, parent_factor, tail,
     child_in, parent_in, front, c_panel, c_corner, c_across, update,
     taken, total, p_panel, p_corner, p_across,
-    matrix, block, strip, wide, whole, local, *sems,
+    matrix, block, strip, low, wide, whole, local, *sems,
 ):
     cube, row, col = lax.axis_index("cube"), lax.axis_index("row"), lax.axis_index("col")
     core, zl, child = cube % 2, cube // 2, cube // 4
@@ -297,7 +303,7 @@
         c_corner, c_across, c_near, c_line, xs, other,
         lambda ref: ref.at[col, zh, x, :, half, core],
         lambda ref: ref.at[zh, x, :, half, core],
-        pairs_of[0:9],
+        True, pairs_of[0:9],
     )
     child_side.corner_out(front.at[0, :, :, 0:LANE])
     child_side.across_out(front.at[0, :, :, LANE:])
@@ -322,7 +328,7 @@
         lambda ref, part: ref.at[part, :, :, :, :, core],
     )
     child_side.prepare_across(x, lambda at_x, part: c_across.at[:, at_x, :, :, core, :, part])
-    child_side.factor(matrix, block, strip, lambda: None)
+    child_side.factor(matrix, block, strip, low, lambda: None)
 
     c_rest.arrived()
     for i in range(4):
@@ -390,7 +396,7 @@
         p_corner, p_across, p_near, p_line, xs, other,
         lambda ref: ref.at[col, zh, x, zl, core],
         lambda ref: ref.at[zh, x, zl, core],
-        pairs_of[9:18],
+        False, pairs_of[9:18],
     )
     sibling.copies[0].wait_recv()
     assemble(0, 0)
@@ -421,7 +427,7 @@
         lambda ref, part: ref.at[part, :, :, :, core],
     )
     parent_side.prepare_across(x, lambda at_x, part: p_across.at[:, at_x, :, core, :, part])
-    parent_side.factor(matrix, block, strip, lambda: sibling.copies[3].start())
+    parent_side.factor(matrix, block, strip, low, lambda: sibling.copies[3].start())
 
     p_rest.arrived()
     rows = cycles * SUB
@@ -488,6 +494,7 @@
             pltpu.VMEM((WIDTH, WIDTH), F32),
             pltpu.VMEM((LANE, LANE), F32),
             pltpu.VMEM((LANE, WIDTH), F32),
+            pltpu.VMEM((WIDTH, LANE), F32),
             pltpu.VMEM((cycles * CHILDREN * SUB, WIDTH), F32),
             pltpu.VMEM((cycles * CHILDREN * SUB, WIDTH), F32),
             pltpu.SemaphoreType.DMA((3,)),

time: 95.8 us -> 94.1 us (0.982)
  Pallas kernels: 95.1 us -> 93.3 us
    pallas_call x1, Pallas kernels: 93.1 us -> 91.4 us  [shards(): pl.pallas_call(kernel, out_shape=(jax.ShapeDtypeStruct((cycles * CHILDREN...]
where the time goes in v5:
time: 94.1 us; the launch traced here: 93.9 us
  Pallas kernels  93.3 us (99%)
    pallas_call x1, Pallas kernels, shards(): pl.pallas_call(kernel, out_shape=(jax.ShapeDtypeStruct((cycles * CHILDREN...  91.4 us
    pallas_call x1, Pallas kernels, shards(): pl.pallas_call(hand_on, out_shape=tuple((jax.ShapeDtypeStruct(value.shape...  1.94 us

profile of v5, /device:TPU:1, one launch (start us, length us, event | category | flops | bytes accessed | tf_op | source)
XLA Modules:
  0.0 93.9 jit_solution(3118439831612078210)
XLA Ops:
  0.6 91.4 %fronts.1 = (f32[192,128]{1,0:T(8,128)}, f32[96,128]{1,0:T(8,128)}, f32[968,128]{1,0:T(8,128)}) custom-call(s32[2,11]{1,0:T(2,128)} %border_map.1, f32[2304,128]{1,0:T(8,128)} %bitcast.9, f32[1152,128]{1,0:T(8,128)} %bitcast.10), custom_call_target="tpu_custom_call" | custom-call | tf_op jit(solution)/shard_map/fronts/pallas_call | solution.py:472
  92.0 1.9 %hand_on.1 = (f32[192,128]{1,0:T(8,128)}, f32[96,128]{1,0:T(8,128)}, f32[968,128]{1,0:T(8,128)}) custom-call(f32[192,128]{1,0:T(8,128)} %get-tuple-element.9.first, f32[96,128]{1,0:T(8,128)} %get-tuple-element.10.second, f32[968,128]{1,0:T(8,128)} %get-tuple-element.11.third), custom_call_target="tpu_custom_call" | custom-call | tf_op jit(solution)/shard_map/hand_on/pallas_call | solution.py:510

commit v6 on v5

--- a/solution.py
+++ b/solution.py
@@ -83,30 +83,37 @@
 
 def inverse_factor(matrix, block, strip, low, midway, after):
     blocks = WIDTH // LANE
-    low[...] = jnp.zeros(low.shape, F32)
-    strip[...] = jnp.zeros(strip.shape, F32)
-
-    def body(k, carry):
-        here = pl.ds(pl.multiple_of(k * LANE, LANE), LANE)
-        share = matrix[here, here] - mm(low[here, :], strip[:, here])
+    for k in range(blocks):
+        here = slice(k * LANE, (k + 1) * LANE)
+        share = matrix[here, here]
+        if k:
+            share = share - mm(low[here, :], strip[:, here])
         tiles = [share[SUB * i : SUB * (i + 1), :] for i in range(LANE // SUB)]
-        for i in range(1, blocks):
+        for i in range(k, blocks) if k else ():
             below = slice(i * LANE, (i + 1) * LANE)
             matrix[below, :] = matrix[below, :] - mm(low[below, :], strip[...])
         diagonal_inverse(tiles, block, lambda: midway(k))
         after(k)
         strip[...] = mm(block[...], matrix[here, :])
         strip[:, here] = block[...]
-        for i in range(1, blocks):
+        for i in range(k + 1, blocks):
             below = slice(i * LANE, (i + 1) * LANE)
-            low[below, :] = jnp.where(k < i, mm_t(matrix[below, here], block[...]), 0.0)
-            matrix[below, here] = jnp.where(k < i, 0.0, matrix[below, here])
+            low[below, :] = mm_t(matrix[below, here], block[...])
+            matrix[below, here] = jnp.zeros((LANE, LANE), F32)
         for i in range(blocks):
             columns = slice(i * LANE, (i + 1) * LANE)
-            matrix[here, columns] = jnp.where(k >= i, strip[:, columns], 0.0)
-        return carry
-
-    lax.fori_loop(0, blocks, body, 0)
+            if k >= i:
+                matrix[here, columns] = strip[:, columns]
+            else:
+                matrix[here, columns] = jnp.zeros((LANE, LANE), F32)
+
+
+def only(chosen):
+    def run(action):
+        if chosen:
+            action()
+
+    return run
 
 
 class Sends:
@@ -211,7 +218,7 @@
         fill(matrix, self.corner, 0, 1)
 
         def midway(k):
-            @pl.when(k == 0)
+            @only(k == 0)
             def _():
                 self.dx1.arrived()
                 self.dc1.start()
@@ -220,13 +227,13 @@
                     self.ring.start()
                 also()
 
-            @pl.when(k == 3)
+            @only(k == 3)
             def _():
                 self.on.arrived()
                 self.ac.copies[3].start()
 
         def after(k):
-            @pl.when(k == 0)
+            @only(k == 0)
             def _():
                 if self.late:
                     self.az.arrived()
@@ -234,13 +241,13 @@
                 self.dc1.arrived()
                 fill(matrix, self.corner, 1, 4)
 
-            @pl.when(k == 1)
+            @only(k == 1)
             def _():
                 for copy in self.ring.copies[:2]:
                     copy.wait_recv()
                 self.on.start()
 
-            @pl.when(k == 2)
+            @only(k == 2)
             def _():
                 for copy in self.ring.copies[2:]:
                     copy.wait_recv()

time: 94.1 us -> 93 us (0.988)
  Pallas kernels: 93.3 us -> 92.3 us
    pallas_call x1, Pallas kernels: 91.4 us -> 90.3 us  [shards(): pl.pallas_call(kernel, out_shape=(jax.ShapeDtypeStruct((cycles * CHILDREN...]
where the time goes in v6:
time: 93 us; the launch traced here: 92.9 us
  Pallas kernels  92.3 us (99%)
    pallas_call x1, Pallas kernels, shards(): pl.pallas_call(kernel, out_shape=(jax.ShapeDtypeStruct((cycles * CHILDREN...  90.3 us
    pallas_call x1, Pallas kernels, shards(): pl.pallas_call(hand_on, out_shape=tuple((jax.ShapeDtypeStruct(value.shape...  1.94 us

profile of v6, /device:TPU:1, one launch (start us, length us, event | category | flops | bytes accessed | tf_op | source)
XLA Modules:
  0.0 92.9 jit_solution(16147498634805852884)
XLA Ops:
  0.6 90.3 %fronts.1 = (f32[192,128]{1,0:T(8,128)}, f32[96,128]{1,0:T(8,128)}, f32[968,128]{1,0:T(8,128)}) custom-call(s32[2,11]{1,0:T(2,128)} %border_map.1, f32[2304,128]{1,0:T(8,128)} %bitcast.9, f32[1152,128]{1,0:T(8,128)} %bitcast.10), custom_call_target="tpu_custom_call" | custom-call | tf_op jit(solution)/shard_map/fronts/pallas_call | solution.py:479
  91.0 1.9 %hand_on.1 = (f32[192,128]{1,0:T(8,128)}, f32[96,128]{1,0:T(8,128)}, f32[968,128]{1,0:T(8,128)}) custom-call(f32[192,128]{1,0:T(8,128)} %get-tuple-element.9.first, f32[96,128]{1,0:T(8,128)} %get-tuple-element.10.second, f32[968,128]{1,0:T(8,128)} %get-tuple-element.11.third), custom_call_target="tpu_custom_call" | custom-call | tf_op jit(solution)/shard_map/hand_on/pallas_call | solution.py:517
